TPU v7x, 32 devices: a whole 2x2x4 slice. The times are simulated.
32 devices in a mesh: fsdp: 2 (over x), ctx: 4 (over y, core), tp: 4 (over z).
Axes of the slice: x: 2, y: 2, z: 4, core: 2. Of those that a mesh axis runs over, the one named last changes fastest.
Arguments:
- inputs: bfloat16 [8, 1024, 768], P('fsdp', ('ctx', 'tp')), may hold values from -6 to 6
- segments: int32 [8, 1024], P('fsdp', ('ctx', 'tp')), may hold values from 0 to 15, never falling along the last dimension, each value on 1 to 512 neighbouring positions
- ln1_gain: float32 [768], replicated, may hold values from 0.25 to 1.75
- ln1_bias: float32 [768], replicated, may hold values from -3 to 3
- query_key_value_weight: bfloat16 [768, 3, 768], P(('fsdp', 'ctx'), None, 'tp'), may hold values from -0.21875 to 0.21875
- b_qv: float32 [2, 768], P(None, 'tp'), may hold values from -3 to 3
- output_weight: bfloat16 [768, 768], P('tp', ('fsdp', 'ctx')), may hold values from -0.625 to 0.625
- output_bias: float32 [768], replicated, may hold values from -3 to 3
- ln2_gain: float32 [768], replicated, may hold values from 0.25 to 1.75
- ln2_bias: float32 [768], replicated, may hold values from -3 to 3
- up_weight: bfloat16 [768, 3072], P(('fsdp', 'ctx'), 'tp'), may hold values from -0.21875 to 0.21875
- up_bias: float32 [3072], P('tp'), may hold values from -3 to 3
- down_weight: bfloat16 [3072, 768], P('tp', ('fsdp', 'ctx')), may hold values from -0.109375 to 0.109375
- down_bias: float32 [768], replicated, may hold values from -3 to 3
- out_grad: bfloat16 [8, 1024, 768], P('fsdp', ('ctx', 'tp')), may hold values from -6 to 6
Outputs:
- output: bfloat16 [8, 1024, 768], P('fsdp', ('ctx', 'tp'))
- input_grad: float32 [8, 1024, 768], P('fsdp', ('ctx', 'tp'))
- grad_ln1_gain: float32 [768], replicated
- grad_ln1_bias: float32 [768], replicated
- grad_qkv: float32 [768, 3, 768], P(('fsdp', 'ctx'), None, 'tp')
- grad_qkv_bias: float32 [2, 768], P(None, 'tp')
- grad_out: float32 [768, 768], P('tp', ('fsdp', 'ctx'))
- grad_out_bias: float32 [768], replicated
- grad_ln2_gain: float32 [768], replicated
- grad_ln2_bias: float32 [768], replicated
- grad_up: float32 [768, 3072], P(('fsdp', 'ctx'), 'tp')
- grad_up_bias: float32 [3072], P('tp')
- grad_down: float32 [3072, 768], P('tp', ('fsdp', 'ctx'))
- grad_down_bias: float32 [768], replicated
Inputs may be any that keep to these rules, and one draw needn't show every extreme that they name: `segments`: segment numbers never fall along a sequence; each number covers 1 to 512 positions of a sequence, one exactly 512.
All inputs are finite; a program needn't handle non-finite values.
Results may differ from a plain program's by a relative error of at most 0.011.
Values may be sent and summed in bfloat16 or wider, within the bound.
No kernel may reach another device: no remote copies, remote signals or barrier semaphores. Data moves between devices by JAX's collectives and lax.ppermute only.
A program may use at most 128 MiB of HBM per device.

v0:
```python
from functools import partial

import jax
import jax.numpy as jnp
from jax import lax
from jax.experimental import pallas as pl
from jax.experimental.pallas import tpu as pltpu
from jax.sharding import PartitionSpec as P

DH = 64
EPS = 1e-06
BF = jnp.bfloat16
F32 = jnp.float32
NEG = -1e30
SPARE = 8
VMEM = pl.BlockSpec(memory_space=pltpu.VMEM)
SMEM = pl.BlockSpec(memory_space=pltpu.SMEM)


def after(x, *deps):
    return lax.optimization_barrier((x,) + deps)[0]


def xor_swap(x, axis, k):
    n = lax.axis_size(axis)
    return lax.ppermute(x, axis, [(i, i ^ k) for i in range(n)])


def turn_pairs(n, k):
    return [(a * n + b, b * n + (a ^ k)) for a in range(n) for b in range(n)]


def send_turned(x, k):
    return lax.ppermute(x, ("ctx", "tp"), turn_pairs(lax.axis_size("tp"), k))


def send_back(x, k):
    pairs = turn_pairs(lax.axis_size("tp"), k)
    return lax.ppermute(x, ("ctx", "tp"), [(d, s) for s, d in pairs])


def hop_pairs(n, k):
    pairs = []
    for a in range(n):
        for q in range(n):
            f, low = (q ^ k) // 2, (q ^ k) % 2
            pairs.append((a * n + q, ((a // 2) * 2 + low) * n + (a ^ (2 * f))))
    return pairs


def scatter_blocks(pieces, *late):
    n = lax.axis_size("tp")
    y, q = lax.axis_index("ctx") // 2, lax.axis_index("tp")
    split = pieces.reshape((2, 2) + pieces.shape[1:])
    got = xor_swap(pick(split, y ^ 1), "ctx", 2)
    four = after(jnp.concatenate([pick(split, y), got], 0), *late)
    return [lax.ppermute(pick(four, q ^ k), ("ctx", "tp"), hop_pairs(n, k)) for k in range(n)]


def rows_over_z(arr):
    return lax.all_to_all(arr, "tp", 0, 0, tiled=True)


def place(pieces, first):
    out = jnp.zeros((len(pieces),) + pieces[0].shape, pieces[0].dtype)
    for k, piece in enumerate(pieces):
        out = lax.dynamic_update_index_in_dim(out, piece, first ^ k, 0)
    return out


def pick(arr, index):
    return lax.dynamic_index_in_dim(arr, index, 0, keepdims=False)


def gather_ctx(own):
    half = jnp.concatenate([own, xor_swap(own, "ctx", 2)], 0)
    return half, xor_swap(half, "ctx", 1)


def weight_over_x(rows):
    if lax.axis_size("fsdp") == 2:
        got = xor_swap(rows, "fsdp", 1)
        first = lax.axis_index("fsdp") == 0
        return jnp.stack([jnp.where(first, rows, got), jnp.where(first, got, rows)])
    every = lax.all_gather(rows, "fsdp", axis=0, tiled=True)
    return every.reshape(2, -1, every.shape[1])


def nt(a, b):
    return lax.dot_general(a, b, (((1,), (1,)), ((), ())), preferred_element_type=F32)


def nn(a, b):
    return lax.dot_general(a, b, (((1,), (0,)), ((), ())), preferred_element_type=F32)


def tn(a, b):
    return lax.dot_general(a, b, (((0,), (0,)), ((), ())), preferred_element_type=F32)


def params(limit, steps=None):
    return pltpu.CompilerParams(vmem_limit_bytes=limit << 20)


def cost(micros, nbytes):
    return pl.CostEstimate(
        flops=int(micros * 0.2 * 10**9), transcendentals=0, bytes_accessed=1024
    )


def normed(x):
    n = x.shape[-1]
    centred = x - jnp.sum(x, -1, keepdims=True) * (1.0 / n)
    rstd = lax.rsqrt(jnp.sum(centred * centred, -1, keepdims=True) * (1.0 / n) + EPS)
    return centred * rstd, rstd


def normed_back(grad, normal, rstd, gain):
    n = grad.shape[-1]
    scaled = grad * gain
    one = jnp.sum(scaled, -1, keepdims=True) * (1.0 / n)
    two = jnp.sum(scaled * normal, -1, keepdims=True) * (1.0 / n)
    return rstd * (scaled - one - normal * two)


def bias_row(ref, row):
    parts = ref[row : row + 3, :].astype(F32)
    return parts[0:1] + parts[1:2] + parts[2:3]


def qkv_kernel(
    cols,
    xo_ref,
    xp_ref,
    vec_ref,
    b_ref,
    w_ref,
    qkv_ref,
    seg_ref,
    lo_ref,
    hi_ref,
):
    first, pieces = xo_ref.shape[0], xo_ref.shape[1]
    thin, width = qkv_ref.shape[2], xo_ref.shape[3]
    half = width // 2
    b = bias_row(b_ref, 0)
    for i in range(2 * first):
        x_ref = xo_ref if i < first else xp_ref
        normal, _ = normed(x_rows(x_ref, i % first, thin).astype(F32))
        xa = (normal * vec_ref[0:1, :] + vec_ref[1:2, :]).astype(BF)
        mixed = nn(xa[:, :half], w_ref[0, :, : 3 * cols]) + nn(xa[:, half:], w_ref[1, :, : 3 * cols])
        parts = (
            mixed[:, :cols] + b[:, :cols],
            mixed[:, cols : 2 * cols],
            mixed[:, 2 * cols :] + b[:, cols : 2 * cols],
        )
        for c, part in enumerate(parts):
            put_lanes(qkv_ref, i, c, part)
        labels = [
            x_ref[i % first, k, thin : thin + SPARE, :thin].astype(F32)[0:1, :]
            for k in range(pieces)
        ]
        labels = jnp.concatenate(labels, 1)
        seg_ref[:, i * pieces * thin : (i + 1) * pieces * thin] = jnp.broadcast_to(
            labels, (8, pieces * thin)
        )
        lo_ref[i] = jnp.min(labels).astype(jnp.int32)
        hi_ref[i] = jnp.max(labels).astype(jnp.int32)


def qkv(xo, xp, vec, b, w, cols, thin):
    first, pieces, _, _ = xo.shape
    bound = jax.ShapeDtypeStruct((2 * first,), jnp.int32)
    return pl.pallas_call(
        partial(qkv_kernel, cols),
        out_shape=(
            jax.ShapeDtypeStruct((2 * first, pieces, thin, 4 * cols), BF),
            jax.ShapeDtypeStruct((8, 2 * first * pieces * thin), F32),
            bound,
            bound,
        ),
        in_specs=[VMEM] * 5,
        out_specs=(VMEM,) * 2 + (SMEM,) * 2,
        compiler_params=params(12),
        cost_estimate=cost(4, 6 << 20),
        name="qkv",
    )(xo, xp, vec, b, w)


def head_mask(h, width):
    lane = lax.broadcasted_iota(jnp.int32, (1, width), 1)
    return (lane >= h * DH) & (lane < (h + 1) * DH)


def only_head(x, h):
    return jnp.where(head_mask(h, x.shape[1]), x, jnp.zeros_like(x))


def x_rows(ref, i, thin):
    return ref[i, :, :thin, :].reshape(-1, ref.shape[3])


def group(ref, i):
    return ref[i].reshape(ref.shape[1] * ref.shape[2], ref.shape[3])


def put_rows(ref, i, value):
    ref[i] = value.astype(ref.dtype).reshape(ref.shape[1:])


def lanes_of(ref, part):
    cols = ref.shape[-1] // 4
    wide = ref.shape[-1] // 3
    return slice(part * wide, part * wide + cols)


def part_rows(ref, i, part):
    value = ref[i, :, :, lanes_of(ref, part)]
    return value.reshape(-1, value.shape[-1])


def put_lanes(ref, i, part, value):
    ref[i, :, :, lanes_of(ref, part)] = value.astype(ref.dtype).reshape(
        ref.shape[1:3] + value.shape[1:]
    )


def turned(x):
    return jnp.transpose(x.astype(F32)).astype(x.dtype)


def with_blocks(lo_ref, hi_ref, list_ref, i, groups, work):
    count = jnp.int32(0)
    for j in range(groups):
        on = (hi_ref[i] >= lo_ref[j]) & (lo_ref[i] <= hi_ref[j])

        @pl.when(on)
        def _():
            list_ref[count] = j

        count = count + on.astype(jnp.int32)
    for number in range(1, groups + 1):

        @pl.when(count == number)
        def _():
            work([list_ref[t] for t in range(number)])


def put_projected(kept_ref, sent_ref, i, project):
    first = kept_ref.shape[0]
    out = kept_ref if i < first else sent_ref
    half = out.shape[3] // 2
    for part in range(2):
        out[i % first, :, :, part * half : (part + 1) * half] = (
            project(part).astype(out.dtype).reshape(out.shape[1:3] + (half,))
        )


def attend_kernel(
    heads,
    lo_ref,
    hi_ref,
    qkv_ref,
    segr_ref,
    w_ref,
    att_ref,
    lse_ref,
    kept_ref,
    sent_ref,
    kk,
    vt,
    ow,
    segc_ref,
    list_ref,
):
    groups = qkv_ref.shape[0]
    n = qkv_ref.shape[1] * qkv_ref.shape[2]
    cols = qkv_ref.shape[3] // 4
    segc_ref[...] = jnp.transpose(segr_ref[...])
    ow[...] = w_ref[:, :, 3 * cols :]
    for i in range(groups):
        kk[i * n : (i + 1) * n, :] = part_rows(qkv_ref, i, 1)
        vt[i] = turned(part_rows(qkv_ref, i, 2))

    def per_query(i, carry):
        qs = pl.ds(pl.multiple_of(i * n, n), n)

        def work(js):
            seg_q = segr_ref[0:1, qs]
            q = part_rows(qkv_ref, i, 0) * jnp.asarray(0.125, BF)
            places = [pl.ds(pl.multiple_of(j * n, n), n) for j in js]
            same = [segc_ref[ks, 0:1] == seg_q for ks in places]
            outs = []
            for h in range(heads):
                qh = only_head(q, h)
                scores = [
                    jnp.where(mask, nt(kk[ks, :], qh), NEG) for ks, mask in zip(places, same)
                ]
                top = [jnp.max(s, 0, keepdims=True) for s in scores]
                top = sum_of(top, jnp.maximum)
                total, out = [], []
                for s, j in zip(scores, js):
                    p = jnp.exp(s - top)
                    total.append(jnp.sum(p, 0, keepdims=True))
                    out.append(nn(vt[j, h * DH : (h + 1) * DH, :], p.astype(BF)))
                total = sum_of(total, jnp.add)
                outs.append(sum_of(out, jnp.add) * (1.0 / total))
                lse_ref[h : h + 1, qs] = top + jnp.log(total)
            out = jnp.transpose(jnp.concatenate(outs, 0))
            put_rows(att_ref, i, jnp.where(segc_ref[qs, 0:1] > 0, out, 0.0))

        with_blocks(lo_ref, hi_ref, list_ref, i, groups, work)
        return carry

    lax.fori_loop(0, groups, per_query, 0)
    for i in range(groups):
        att = group(att_ref, i)
        put_projected(kept_ref, sent_ref, i, lambda part: nt(att, ow[part]))


def sum_of(values, join):
    total = values[0]
    for value in values[1:]:
        total = join(total, value)
    return total


def attend(lo, hi, mixed, segr, w):
    groups, pieces, thin, _ = mixed.shape
    cols = mixed.shape[3] // 4
    heads = cols // DH
    n, rows = pieces * thin, groups * pieces * thin
    width = 2 * w.shape[1]
    return pl.pallas_call(
        partial(attend_kernel, heads),
        out_shape=(
            jax.ShapeDtypeStruct((groups, pieces, thin, cols), BF),
            jax.ShapeDtypeStruct((8, rows), F32),
            jax.ShapeDtypeStruct((groups // 2, pieces, thin, width), F32),
            jax.ShapeDtypeStruct((groups // 2, pieces, thin, width), BF),
        ),
        in_specs=[SMEM, SMEM] + [VMEM] * 3,
        out_specs=(VMEM,) * 4,
        scratch_shapes=[
            pltpu.VMEM((rows, cols), BF),
            pltpu.VMEM((groups, cols, n), BF),
            pltpu.VMEM((2, width // 2, cols), BF),
            pltpu.VMEM((rows, 8), F32),
            pltpu.SMEM((groups,), jnp.int32),
        ],
        compiler_params=params(16),
        cost_estimate=cost(11, 8 << 20),
        name="attend",
    )(lo, hi, mixed, segr, w)


def attend_back_kernel(
    heads,
    lo_ref,
    hi_ref,
    qkv_ref,
    att_ref,
    lse_ref,
    db_ref,
    dp_ref,
    segr_ref,
    w_ref,
    dmix_ref,
    kept_ref,
    sent_ref,
    kt,
    kk,
    vv,
    do_ref,
    delta,
    ak,
    av,
    ow,
    kw,
    segc_ref,
    list_ref,
):
    groups = qkv_ref.shape[0]
    n = qkv_ref.shape[1] * qkv_ref.shape[2]
    cols = qkv_ref.shape[3] // 4
    half = w_ref.shape[1]
    segc_ref[...] = jnp.transpose(segr_ref[...])
    ow[...] = w_ref[:, :, 3 * cols :]
    kw[...] = w_ref[:, :, cols : 2 * cols]
    ak[...] = jnp.zeros_like(ak)
    av[...] = jnp.zeros_like(av)
    for i in range(groups):
        rows = slice(i * n, (i + 1) * n)
        kk[rows, :] = part_rows(qkv_ref, i, 1)
        vv[rows, :] = part_rows(qkv_ref, i, 2)
        kt[i] = turned(part_rows(qkv_ref, i, 1))
        grad = group(db_ref, i) if i < groups // 2 else group(dp_ref, i - groups // 2)
        out_back = nn(grad[:, :half], ow[0]) + nn(grad[:, half:], ow[1])
        do = jnp.where(segc_ref[rows, 0:1] > 0, out_back, 0.0).astype(BF)
        do_ref[rows, :] = do
        prod = jnp.transpose(do.astype(F32) * group(att_ref, i).astype(F32))
        for h in range(heads):
            delta[h : h + 1, rows] = jnp.sum(prod[h * DH : (h + 1) * DH, :], 0, keepdims=True)

    def per_query(i, carry):
        qs = pl.ds(pl.multiple_of(i * n, n), n)

        def work(js):
            seg_q = segr_ref[0:1, qs]
            q = part_rows(qkv_ref, i, 0) * jnp.asarray(0.125, BF)
            do = do_ref[qs, :]
            qh = [only_head(q, h) for h in range(heads)]
            dh = [only_head(do, h) for h in range(heads)]
            dq = [[] for _ in range(heads)]
            for j in js:
                ks = pl.ds(pl.multiple_of(j * n, n), n)
                same = segc_ref[ks, 0:1] == seg_q
                dk, dv = [], []
                for h in range(heads):
                    s = jnp.where(same, nt(kk[ks, :], qh[h]), NEG)
                    p = jnp.exp(s - lse_ref[h : h + 1, qs])
                    ds = (p * (nt(vv[ks, :], dh[h]) - delta[h : h + 1, qs])).astype(BF)
                    dv.append(nn(p.astype(BF), dh[h]))
                    dk.append(nn(ds, qh[h]))
                    dq[h].append(nn(kt[j, h * DH : (h + 1) * DH, :], ds))
                ak[ks, :] += sum_of(dk, jnp.add)
                av[ks, :] += sum_of(dv, jnp.add)
            dq = jnp.concatenate([sum_of(parts, jnp.add) for parts in dq], 0)
            put_lanes(dmix_ref, i, 0, jnp.transpose(dq) * 0.125)

        with_blocks(lo_ref, hi_ref, list_ref, i, groups, work)
        return carry

    lax.fori_loop(0, groups, per_query, 0)
    for i in range(groups):
        rows = slice(i * n, (i + 1) * n)
        dq = part_rows(dmix_ref, i, 0)
        dk = ak[rows, :].astype(BF)
        dv = av[rows, :].astype(BF)
        put_lanes(dmix_ref, i, 1, dk)
        put_lanes(dmix_ref, i, 2, dv)

        def project(part):
            dx = nt(dq, w_ref[part, :, :cols]) + nt(dk, kw[part])
            return dx + nt(dv, w_ref[part, :, 2 * cols : 3 * cols])

        put_projected(kept_ref, sent_ref, i, project)


def attend_back(lo, hi, mixed, att, lse, db, dp, segr, w):
    groups, pieces, thin, cols = att.shape
    heads = cols // DH
    n, rows = pieces * thin, groups * pieces * thin
    width = 2 * w.shape[1]
    return pl.pallas_call(
        partial(attend_back_kernel, heads),
        out_shape=(
            jax.ShapeDtypeStruct(mixed.shape, BF),
            jax.ShapeDtypeStruct((groups // 2, pieces, thin, width), F32),
            jax.ShapeDtypeStruct((groups // 2, pieces, thin, width), BF),
        ),
        in_specs=[SMEM, SMEM] + [VMEM] * 7,
        out_specs=(VMEM,) * 3,
        scratch_shapes=[
            pltpu.VMEM((groups, cols, n), BF),
            pltpu.VMEM((rows, cols), BF),
            pltpu.VMEM((rows, cols), BF),
            pltpu.VMEM((rows, cols), BF),
            pltpu.VMEM((8, rows), F32),
            pltpu.VMEM((rows, cols), F32),
            pltpu.VMEM((rows, cols), F32),
            pltpu.VMEM((2, width // 2, cols), BF),
            pltpu.VMEM((2, width // 2, cols), BF),
            pltpu.VMEM((rows, 8), F32),
            pltpu.SMEM((groups,), jnp.int32),
        ],
        compiler_params=params(18),
        cost_estimate=cost(70, 12 << 20),
        name="attend_back",
    )(lo, hi, mixed, att, lse, db, dp, segr, w)


def middle_kernel(s_ref, got_ref, x_ref, vec_ref, mid_ref, xb_ref):
    n, _, thin, width = s_ref.shape
    for i in range(n):
        x = x_rows(x_ref, i, thin).astype(F32)
        mid = group(s_ref, i).astype(F32) + group(got_ref, n - 1 - i).astype(F32) + x + vec_ref[0:1, :]
        put_rows(mid_ref, i, mid)
        normal, _ = normed(mid)
        put_rows(xb_ref, i, normal * vec_ref[1:2, :] + vec_ref[2:3, :])


def middle_rows(s, got, x, vec):
    return pl.pallas_call(
        middle_kernel,
        out_shape=(jax.ShapeDtypeStruct(s.shape, F32), jax.ShapeDtypeStruct(s.shape, BF)),
        in_specs=[VMEM] * 4,
        out_specs=(VMEM,) * 2,
        compiler_params=params(8),
        cost_estimate=cost(2, 4 << 20),
        name="middle_rows",
    )(s, got, x, vec)


def middle_back_kernel(s_ref, got_ref, mid_ref, g_ref, vec_ref, dmid_ref, db_ref, sum_ref):
    n = s_ref.shape[0]
    for i in range(n):
        dxb = group(s_ref, i).astype(F32) + group(got_ref, n - 1 - i).astype(F32)
        normal, rstd = normed(group(mid_ref, i))
        grad = group(g_ref, i).astype(F32)
        dmid = grad + normed_back(dxb, normal, rstd, vec_ref[...])
        low = dmid.astype(BF)
        put_rows(dmid_ref, i, dmid)
        put_rows(db_ref, i, low)
        if i == 0:
            sum_ref[0:1, :] = jnp.sum(low.astype(F32), 0, keepdims=True)
            sum_ref[1:2, :] = jnp.sum(dxb * normal, 0, keepdims=True)
            sum_ref[2:3, :] = jnp.sum(dxb, 0, keepdims=True)
            sum_ref[3:4, :] = jnp.sum(grad, 0, keepdims=True)


def middle_back(s, got, mid, g, vec):
    return pl.pallas_call(
        middle_back_kernel,
        out_shape=(
            jax.ShapeDtypeStruct(s.shape, F32),
            jax.ShapeDtypeStruct(s.shape, BF),
            jax.ShapeDtypeStruct((4, s.shape[-1]), F32),
        ),
        in_specs=[VMEM] * 5,
        out_specs=(VMEM,) * 3,
        compiler_params=params(8),
        cost_estimate=cost(2, 5 << 20),
        name="middle_back",
    )(s, got, mid, g, vec)


def add_kernel(kept_ref, got_ref, *out_refs):
    at = 0
    for ref in out_refs:
        for i in range(ref.shape[0]):
            put_rows(ref, i, group(kept_ref, at) + group(got_ref, at).astype(F32))
            at += 1


def core_sum(kept, sent, split):
    got = xor_swap(sent, "ctx", 1)
    return pl.pallas_call(
        add_kernel,
        out_shape=[jax.ShapeDtypeStruct((n,) + kept.shape[1:], BF) for n in split],
        in_specs=[VMEM] * 2,
        out_specs=[VMEM] * len(split),
        compiler_params=params(6),
        cost_estimate=cost(1, 4 << 20),
        name="add_rows",
    )(kept, got)


def first_back_kernel(
    s_ref, got_ref, x_ref, dmid_ref, mid_ref, mlp_ref, mlpgot_ref, vec_ref, out_ref
):
    thin = s_ref.shape[2]
    pieces = out_ref.shape[0]
    result = group(mid_ref, 0) + group(mlp_ref, 0).astype(F32) + group(mlpgot_ref, 0).astype(F32)
    result = result + vec_ref[1:2, :]
    out_ref[:, :thin, :] = result.astype(BF).reshape(pieces, thin, -1)
    dxa = group(s_ref, 0).astype(F32) + group(got_ref, 0).astype(F32)
    normal, rstd = normed(x_rows(x_ref, 0, thin).astype(F32))
    grad = group(dmid_ref, 0) + normed_back(dxa, normal, rstd, vec_ref[0:1, :])
    out_ref[:, thin:, :] = grad.astype(BF).reshape(pieces, thin, -1)


def first_back(s, got, x, dmid, mid, mlp, mlpgot, vec):
    _, pieces, thin, width = s.shape
    return pl.pallas_call(
        first_back_kernel,
        out_shape=jax.ShapeDtypeStruct((pieces, 2 * thin, width), BF),
        in_specs=[VMEM] * 8,
        out_specs=VMEM,
        compiler_params=params(8),
        cost_estimate=cost(20, 6 << 20),
        name="first_back",
    )(s, got, x, dmid, mid, mlp, mlpgot, vec)


def pieces_kernel(own_ref, got_ref, vec_ref, out_ref):
    blocks, r = out_ref.shape[0], out_ref.shape[1] - SPARE
    for b in range(blocks):
        part = slice(b * r, (b + 1) * r)
        out_ref[b, :r, :] = (own_ref[part, :].astype(F32) + got_ref[part, :].astype(F32)).astype(BF)
        last = slice(blocks * r, blocks * r + 2)
        out_ref[b, r : r + 2, :] = (
            own_ref[last, :].astype(F32) + got_ref[last, :].astype(F32)
        ).astype(BF)
        out_ref[b, r + 2 :, :] = vec_ref[...].astype(BF)


def grad_pieces(stay, go, vec, blocks):
    rows = stay.shape[0] - SPARE
    if lax.axis_size("fsdp") == 2 and rows // blocks % 16 == 0:
        return pl.pallas_call(
            pieces_kernel,
            out_shape=jax.ShapeDtypeStruct((blocks, rows // blocks + SPARE, stay.shape[1]), BF),
            in_specs=[VMEM] * 3,
            out_specs=VMEM,
            compiler_params=params(6),
            cost_estimate=cost(1, 2 << 20),
            name="grad_pieces",
        )(stay, xor_swap(go, "fsdp", 1), vec)
    last = lax.psum(stay[rows : rows + 2].astype(F32), "fsdp")
    split = jnp.concatenate([stay[:rows], go[:rows]], 0).reshape(
        lax.axis_size("fsdp"), -1, stay.shape[1]
    )
    own = lax.psum_scatter(split.astype(F32), "fsdp", scatter_dimension=0, tiled=False)
    own = own.reshape(blocks, -1, own.shape[-1])
    small = jnp.concatenate([last, vec], 0)
    small = jnp.broadcast_to(small, (blocks,) + small.shape)
    return jnp.concatenate([own, small], 1).astype(BF)


def weight_part(ref, part):
    w = ref[:, part]
    return w.reshape(w.shape[0] * w.shape[1], w.shape[2])


def mlp_kernel(
    xo_ref,
    xp_ref,
    go_ref,
    gp_ref,
    m_ref,
    b_ref,
    hidden_ref,
    dpre_ref,
    kept_ref,
    sent_ref,
):
    first = xo_ref.shape[0]
    b = bias_row(b_ref, 3)
    for i in range(2 * first):
        own = i < first
        pre = nn(group(xo_ref if own else xp_ref, i % first), weight_part(m_ref, 0)) + b
        dhidden = nn(group(go_ref if own else gp_ref, i % first), weight_part(m_ref, 1))
        share = 0.5 * (1.0 + lax.erf(pre * (0.5**0.5)))
        density = jnp.exp(pre * pre * -0.5) * ((0.5 / 3.141592653589793) ** 0.5)
        n = pre.shape[0]
        hidden_ref[i * n : (i + 1) * n, :] = (pre * share).astype(BF)
        dpre = (dhidden * (share + pre * density)).astype(BF)
        dpre_ref[i * n : (i + 1) * n, :] = dpre
        put_rows(kept_ref if own else sent_ref, i % first, nt(dpre, weight_part(m_ref, 0)))


def mlp_block(xo, xp, go, gp, m, b):
    blocks, pieces, thin, width = xo.shape
    low = jax.ShapeDtypeStruct((2 * blocks * pieces * thin, m.shape[-1]), BF)
    return pl.pallas_call(
        mlp_kernel,
        out_shape=(low, low, jax.ShapeDtypeStruct(xo.shape, F32), jax.ShapeDtypeStruct(xo.shape, BF)),
        in_specs=[VMEM] * 6,
        out_specs=(VMEM,) * 4,
        compiler_params=params(12),
        cost_estimate=cost(7, 12 << 20),
        name="mlp_block",
    )(xo, xp, go, gp, m, b)


def mlp_grads_kernel(
    xo_ref,
    xp_ref,
    dpre_ref,
    go_ref,
    gp_ref,
    hidden_ref,
    m_ref,
    grad_ref,
    kept_ref,
    sent_ref,
    sum_ref,
):
    first, width = xo_ref.shape[0], xo_ref.shape[3]
    half = width // 2
    rows = dpre_ref.shape[0]
    n = rows // 2

    def half_grads(i, carry):
        lanes = pl.ds(pl.multiple_of(i * half, 128), half)
        xo, xp = (ref[:, :, :, lanes].reshape(n, half) for ref in (xo_ref, xp_ref))
        up = tn(xo, dpre_ref[:n, :]) + tn(xp, dpre_ref[n:, :])
        grad_ref[:, i, 0] = up.astype(BF).reshape((-1,) + grad_ref.shape[3:])
        go, gp = (ref[:, :, :, lanes].reshape(n, half) for ref in (go_ref, gp_ref))
        down = tn(go, hidden_ref[:n, :]) + tn(gp, hidden_ref[n:, :])
        grad_ref[:, i, 1] = down.astype(BF).reshape((-1,) + grad_ref.shape[3:])
        return carry

    lax.fori_loop(0, 2, half_grads, 0)
    size = n // first
    for i in range(2 * first):
        result = nt(hidden_ref[i * size : (i + 1) * size, :], weight_part(m_ref, 1))
        put_rows(kept_ref if i < first else sent_ref, i % first, result)
    sum_ref[...] = jnp.sum(dpre_ref[...].astype(F32), 0, keepdims=True)


def mlp_grads(xo, xp, dpre, go, gp, hidden, m):
    return pl.pallas_call(
        mlp_grads_kernel,
        out_shape=(
            jax.ShapeDtypeStruct((m.shape[0] // 2, 2) + m.shape[1:], BF),
            jax.ShapeDtypeStruct(xo.shape, F32),
            jax.ShapeDtypeStruct(xo.shape, BF),
            jax.ShapeDtypeStruct((1, dpre.shape[1]), F32),
        ),
        in_specs=[VMEM] * 7,
        out_specs=(VMEM,) * 4,
        compiler_params=params(14),
        cost_estimate=cost(6, 12 << 20),
        name="mlp_grads",
    )(xo, xp, dpre, go, gp, hidden, m)


def attend_grads_kernel(
    flip_ref,
    sum_ref,
    norm_ref,
    dmix_ref,
    do_ref,
    dp_ref,
    att_ref,
    kept_ref,
    sent_ref,
    xo_ref,
    xp_ref,
    stay_ref,
    go_ref,
    vec_ref,
    xa,
):
    first, _, thin, width = kept_ref.shape
    rows, cols = att_ref.shape
    half = width // 2
    n = do_ref.shape[0]
    block = rows // (2 * first)
    gain = bias = jnp.zeros((1, width), F32)
    for i in range(2 * first):
        x_ref, g_ref = (xo_ref, kept_ref) if i < first else (xp_ref, sent_ref)
        normal, _ = normed(x_rows(x_ref, i % first, thin).astype(F32))
        xa[i * block : (i + 1) * block, :] = (
            normal * norm_ref[0:1, :] + norm_ref[1:2, :]
        ).astype(BF)
        dx = group(g_ref, i % first).astype(F32)
        gain = gain + jnp.sum(dx * normal, 0, keepdims=True)
        bias = bias + jnp.sum(dx, 0, keepdims=True)
    vec_ref[0:1, :] = gain
    vec_ref[1:2, :] = bias
    totals = [
        jnp.sum(dmix_ref[:, lanes_of(dmix_ref, c)].astype(F32), 0, keepdims=True).astype(BF)
        for c in (0, 2)
    ]

    def half_grads(i, out_ref):
        lanes = pl.ds(pl.multiple_of(i * half, 128), half)
        grads = tn(xa[:, lanes], dmix_ref[...]).astype(BF)
        for c in range(3):
            out_ref[:half, c * cols : (c + 1) * cols] = grads[:, lanes_of(dmix_ref, c)]
        out = tn(do_ref[:, lanes], att_ref[:n, :]) + tn(dp_ref[:, lanes], att_ref[n:, :])
        out_ref[:half, 3 * cols : 4 * cols] = out.astype(BF)
        out_ref[half : half + SPARE, :] = jnp.zeros((SPARE, out_ref.shape[1]), BF)
        for place, total in enumerate(totals):
            out_ref[half : half + 1, place * cols : (place + 1) * cols] = total
        out_ref[half + 1 : half + 2, : sum_ref.shape[1]] = sum_ref[...].astype(BF)

    half_grads(flip_ref[0], stay_ref)
    half_grads(1 - flip_ref[0], go_ref)


def attend_grads(flip, sums, norms, dmix, do, dp, att, kept, sent, xo, xp):
    width = do.shape[1]
    shape = jax.ShapeDtypeStruct((width // 2 + SPARE, 4 * att.shape[1]), BF)
    return pl.pallas_call(
        attend_grads_kernel,
        out_shape=(shape, shape, jax.ShapeDtypeStruct((2, width), F32)),
        in_specs=[SMEM] + [VMEM] * 10,
        out_specs=(VMEM,) * 3,
        scratch_shapes=[pltpu.VMEM((att.shape[0], width), BF)],
        compiler_params=params(14),
        cost_estimate=cost(6, 12 << 20),
        name="attend_grads",
    )(flip, sums, norms, dmix, do, dp, att, kept, sent, xo, xp)


def exact_low(x):
    one = lax.reduce_precision(x, 8, 7)
    two = lax.reduce_precision(x - one, 8, 7)
    return jnp.concatenate([one, two, x - one - two], 0).astype(BF)


def per_device(
    inputs,
    segments,
    ln1_gain,
    ln1_bias,
    query_key_value_weight,
    b_qv,
    output_weight,
    output_bias,
    ln2_gain,
    ln2_bias,
    up_weight,
    up_bias,
    down_weight,
    down_bias,
    out_grad,
):
    z = lax.axis_index("tp")
    ctx = lax.axis_index("ctx")
    planes = lax.axis_size("tp")
    thin, width = inputs.shape[1], inputs.shape[2]
    ds, _, cols = query_key_value_weight.shape
    hidden_cols = up_weight.shape[1]

    vectors = jnp.stack([ln1_gain, ln1_bias, output_bias, ln2_gain, ln2_bias, down_bias])
    rows_of = lambda a: a.reshape(-1, a.shape[-1])

    biases = jnp.pad(b_qv.reshape(1, -1), ((0, 0), (0, width - 2 * cols)))
    biases = [exact_low(biases), exact_low(up_bias.reshape(1, -1)), jnp.zeros((SPARE - 6, width), BF)]
    a_shard = jnp.concatenate(
        [query_key_value_weight.reshape(ds, 3 * cols), jnp.transpose(output_weight)], 1
    )
    a_shard = jnp.concatenate([a_shard] + biases, 0)
    labels = jnp.pad(segments.astype(BF)[:, None, :], ((0, 0), (0, SPARE - 1), (0, width - thin)))
    own = rows_over_z(jnp.concatenate([after(inputs, a_shard), labels, out_grad], 1))
    x_own, g_own = own[:, : thin + SPARE], own[:, thin + SPARE :]
    got = [send_turned(a_shard, k) for k in range(planes)]
    a_rows = place([g[:ds] for g in got], z).reshape(-1, width)
    biases = got[0][ds:]
    w_attn = weight_over_x(a_rows)
    x_pair, x_far = gather_ctx(after(x_own, w_attn)[None])
    g_own = after(g_own, x_pair)[None]

    m_shard = jnp.concatenate([up_weight, jnp.transpose(down_weight)], 0)
    m_shard = send_turned(after(m_shard, a_rows), 0)
    m_all = lax.all_gather(m_shard, ("fsdp", "tp"), axis=0, tiled=True)
    m_all = m_all.reshape(-1, 2, ds, hidden_cols)
    aligned = ds % 16 == 0 and m_all.shape[0] % 2 == 0
    if not aligned:
        m_all = m_all.reshape(2, -1, 2, ds, hidden_cols).transpose(0, 2, 1, 3, 4)
        m_all = m_all.reshape(2, 2, width // 2, hidden_cols)

    mixed, segr, lo, hi = qkv(x_pair, x_far, vectors, biases, w_attn, cols, thin)
    g_got = xor_swap(g_own, "ctx", 2)
    attended, lse, kept, sent = attend(lo, hi, mixed, segr, w_attn)
    g_got, kept, sent = lax.optimization_barrier((g_got, kept, sent))
    g_pair = jnp.concatenate([g_own, g_got], 0)
    g_far = xor_swap(g_pair, "ctx", 1)
    (s,) = core_sum(kept, sent, (2,))
    got = after(xor_swap(s, "ctx", 2), m_all)
    middle, xb_pair = middle_rows(s, got, x_pair, vectors[2:5])
    xb_far = xor_swap(xb_pair, "ctx", 1)

    hidden, dpre, kept, sent = mlp_block(xb_pair, xb_far, g_pair, g_far, m_all, biases)
    (s,) = core_sum(kept, sent, (2,))
    m_grad, mlp_kept, mlp_sent, dpre_sum = mlp_grads(
        xb_pair, xb_far, after(dpre, s), g_pair, g_far, hidden, m_all
    )
    got = xor_swap(s, "ctx", 2)
    mlp_s, mlp_low = core_sum(mlp_kept, after(mlp_sent, got), (1, 1))
    dmid, db_pair, sums_two = middle_back(
        s, after(got, dpre_sum), middle, g_pair, vectors[3:4]
    )
    db_far = xor_swap(db_pair, "ctx", 1)
    if not aligned:
        m_grad = m_grad[0].transpose(1, 0, 2, 3).reshape(2, -1, planes, ds, hidden_cols)
        m_grad = m_grad.transpose(2, 1, 0, 3, 4)
    m_sums = lax.psum_scatter(m_grad, "tp", scatter_dimension=0, tiled=False)
    mlp_got = xor_swap(after(mlp_low, db_far), "ctx", 2)

    dmix, kept, sent = attend_back(
        lo, hi, mixed, attended, lse, db_pair, db_far, segr, w_attn
    )
    s, low = core_sum(kept, after(sent, mlp_got), (1, 1))
    flip = lax.axis_index("fsdp") if lax.axis_size("fsdp") == 2 else 0
    got = xor_swap(low, "ctx", 2)
    g_stay, g_go, sums_one = attend_grads(
        jnp.full((1,), flip, jnp.int32),
        dpre_sum,
        vectors[0:2],
        after(rows_of(dmix), s),
        rows_of(db_pair),
        rows_of(db_far),
        rows_of(attended),
        kept,
        sent,
        x_pair,
        x_far,
    )
    vec = jnp.concatenate([vectors[0:1], vectors[5:6]], 0)
    shared = jnp.concatenate([sums_one, sums_two], 0)
    if lax.axis_size("fsdp") == 2:
        shared = shared + xor_swap(shared, "fsdp", 1)
    else:
        shared = lax.psum(shared, "fsdp")
    shared = shared + xor_swap(shared, "ctx", 1)
    both = first_back(s, after(got, shared), x_pair, dmid, middle, mlp_s, mlp_got, vec)
    shared = after(shared, both)
    shared = shared + xor_swap(shared, "ctx", 2)
    a_low = grad_pieces(g_stay, g_go, shared, planes)

    both = rows_over_z(both)
    output, input_grad = both[:, :thin], both[:, thin:].astype(F32)
    m_z = m_sums
    if lax.axis_size("fsdp") == 2:
        x = lax.axis_index("fsdp")
        m_got = xor_swap(pick(after(m_sums, a_low), x ^ 1), "fsdp", 1)
        m_sums = (pick(m_sums, x).astype(F32) + m_got.astype(F32)).astype(BF)
    else:
        m_sums = lax.psum_scatter(m_sums.astype(F32), "fsdp", scatter_dimension=0, tiled=False)
        m_sums = m_sums.astype(BF)
    m_back = send_back(m_sums.reshape(2 * ds, hidden_cols), 0)
    *got, m_back = lax.optimization_barrier((*scatter_blocks(a_low, m_z, both), m_back))

    g_attn = sum(g.astype(F32) for g in got)
    grad_qkv = g_attn[:ds, : 3 * cols].reshape(ds, 3, cols)
    grad_out = jnp.transpose(g_attn[:ds, 3 * cols :])
    mine, shared = g_attn[ds : ds + 2], g_attn[ds + 2 :]
    g_mlp = m_back.astype(F32)
    grad_up, grad_down = g_mlp[:ds], jnp.transpose(g_mlp[ds:])
    return (
        output,
        input_grad,
        shared[0],
        shared[1],
        grad_qkv,
        mine[0, : 2 * cols].reshape(2, cols),
        grad_out,
        shared[2],
        shared[3],
        shared[4],
        grad_up,
        mine[1, :hidden_cols],
        grad_down,
        shared[5],
    )


def solution(mesh):
    in_specs = (
        P("fsdp", ("ctx", "tp"), None),
        P("fsdp", ("ctx", "tp")),
        P(),
        P(),
        P(("fsdp", "ctx"), None, "tp"),
        P(None, "tp"),
        P("tp", ("fsdp", "ctx")),
        P(),
        P(),
        P(),
        P(("fsdp", "ctx"), "tp"),
        P("tp"),
        P("tp", ("fsdp", "ctx")),
        P(),
        P("fsdp", ("ctx", "tp"), None),
    )
    out_specs = (
        P("fsdp", ("ctx", "tp"), None),
        P("fsdp", ("ctx", "tp"), None),
        P(),
        P(),
        P(("fsdp", "ctx"), None, "tp"),
        P(None, "tp"),
        P("tp", ("fsdp", "ctx")),
        P(),
        P(),
        P(),
        P(("fsdp", "ctx"), "tp"),
        P("tp"),
        P("tp", ("fsdp", "ctx")),
        P(),
    )
    return jax.shard_map(
        per_device, mesh=mesh, in_specs=in_specs, out_specs=out_specs, check_vma=False
    )
```

profile of v0, /device:TPU:1, one launch (start us, length us, event | category | flops | bytes accessed | tf_op | source)
XLA Modules:
  0.0 255.3 jit_solution(7141944769472788848)
XLA Ops:
  11.1 4.6 %collective-permute-start = (bf16[104,768]{1,0:T(8,128)(2,1)S(1)}, bf16[104,768]{1,0:T(8,128)(2,1)S(1)}, u32[]{:S(2)}, u32[]{:S(2)}) collective-permute-start(bf16[104,768]{1,0:T(8,128)(2,1)S(1)} %concatenate.35), channel_id=1, source_target_pairs={{0,0},{1,4},{2,8},{3,12},{4,1},{5,5},{6,9},{7,13},{8,2},{9,6},{10,... | collective-permute-start | bytes 479240 | tf_op jit(solution)/shard_map/ppermute | solution.py:34
  15.8 5.0 %collective-permute-start.2 = (bf16[104,768]{1,0:T(8,128)(2,1)S(1)}, bf16[104,768]{1,0:T(8,128)(2,1)S(1)}, u32[]{:S(2)}, u32[]{:S(2)}) collective-permute-start(bf16[104,768]{1,0:T(8,128)(2,1)S(1)} %concatenate.35), channel_id=1, source_target_pairs={{0,2},{1,6},{2,10},{3,14},{4,3},{5,7},{6,11},{7,15},{8,0},{9,4},{1... | collective-permute-start | bytes 479240 | tf_op jit(solution)/shard_map/ppermute | solution.py:34
  22.5 3.5 %all-to-all-start = ((bf16[4,136,768]{2,1,0:T(8,128)(2,1)}), bf16[4,136,768]{2,1,0:T(8,128)(2,1)S(1)}, u32[]{:S(2)}, u32[]{:S(2)}) async-start(bf16[4,136,768]{2,1,0:T(8,128)(2,1)} %fusion.3), calls=%async_computation | async-start | bytes 1671168 | tf_op jit(solution)/shard_map/all_to_all | solution.py:61
  26.3 2.2 collective-permute-done.3
  28.5 17.8 %collective-permute-start.10 = (bf16[192,768]{1,0:T(8,128)(2,1)S(1)}, bf16[192,768]{1,0:T(8,128)(2,1)S(1)}, u32[]{:S(2)}, u32[]{:S(2)}) collective-permute-start(bf16[192,768]{1,0:T(8,128)(2,1)S(1)} %pad_maximum_fusion.4), channel_id=1, source_target_pairs={{0,0},{1,4},{2,8},{3,12},{4,1},{5,5},{6,9},{7,13},{8,2},{9,6},{10,... | collective-permute-start | bytes 884744 | tf_op jit(solution)/shard_map/ppermute | solution.py:34
  47.5 4.2 %collective-permute-done.10 = bf16[192,768]{1,0:T(8,128)(2,1)S(1)} collective-permute-done((bf16[192,768]{1,0:T(8,128)(2,1)S(1)}, bf16[192,768]{1,0:T(8,128)(2,1)S(1)}, u32[]{:S(2)}, u32[]{:S(2)}) %collective-permute-start.10) | collective-permute-done | bytes 294944 | tf_op jit(solution)/shard_map/ppermute | solution.py:34
  52.5 2.9 %collective-permute-done.4 = bf16[384,768]{1,0:T(8,128)(2,1)S(1)} collective-permute-done((bf16[384,768]{1,0:T(8,128)(2,1)S(1)}, bf16[384,768]{1,0:T(8,128)(2,1)S(1)}, u32[]{:S(2)}, u32[]{:S(2)}) %collective-permute-start.4) | collective-permute-done | bytes 589856 | tf_op jit(solution)/shard_map/ppermute | solution.py:26
  56.8 7.9 %collective-permute-done.5 = bf16[1,4,72,768]{3,2,1,0:T(8,128)(2,1)S(1)} collective-permute-done((bf16[1,4,72,768]{3,2,1,0:T(8,128)(2,1)S(1)}, bf16[1,4,72,768]{3,2,1,0:T(8,128)(2,1)S(1)}, u32[]{:S(2)}, u32[]{:S(2)}) %collective-permute-start.5) | collective-permute-done | bytes 442400 | tf_op jit(solution)/shard_map/ppermute | solution.py:26
  64.8 8.2 %collective-permute-start.6 = (bf16[2,4,72,768]{3,2,1,0:T(8,128)(2,1)S(1)}, bf16[2,4,72,768]{3,2,1,0:T(8,128)(2,1)}, u32[]{:S(2)}, u32[]{:S(2)}) collective-permute-start(bf16[2,4,72,768]{3,2,1,0:T(8,128)(2,1)S(1)} %pad_maximum_fusion.1.xo_ref.x_ref), channel_id=1, source_target_pairs={{0,4},{4,0},{8,12},{12,8},{1,5},{5,1},{9,13},{13,9},{2,6},{6,2},{1... | collective-permute-start | bytes 2654216 | tf_op jit(solution)/shard_map/ppermute | solution.py:26
  75.6 3.7 %qkv.1 = (bf16[4,4,64,768]{3,2,1,0:T(8,128)(2,1)S(1)}, f32[8,1024]{1,0:T(8,128)S(1)}, s32[4]{0:T(128)S(1)}, s32[4]{0:T(128)S(1)}) custom-call(bf16[2,4,72,768]{3,2,1,0:T(8,128)(2,1)S(1)} %pad_maximum_fusion.1.xo_ref.x_ref, bf16[2,4,72,768]{3,2,1,0:T(8,128)(2,1)} %collective-permute-done.6.xp_ref, f32[6,768]{1,0:T(8,128)S(1)} %stack.43.vec_ref, ...), custom_call_target="tpu_custom_call" | custom-call | flops 800000000 | bytes 1024 | tf_op jit(solution)/shard_map/qkv/pallas_call | solution.py:174
  79.3 8.9 %attend.1 = (bf16[4,4,64,192]{3,2,1,0:T(8,128)(2,1)S(1)}, f32[8,1024]{1,0:T(8,128)S(1)}, f32[2,4,64,768]{3,2,1,0:T(8,128)S(1)}, bf16[2,4,64,768]{3,2,1,0:T(8,128)(2,1)S(1)}) custom-call(s32[4]{0:T(128)S(1)} %get-tuple-element.70.lo_ref, s32[4]{0:T(128)S(1)} %get-tuple-element.71.hi_ref, bf16[4,4,64,768]{3,2,1,0:T(8,128)(2,1)S(1)} %get-tuple-element.72.qkv_ref, ...), custom_call_target="tpu_custom_call" | custom-call | flops 2200000000 | bytes 1024 | tf_op jit(solution)/shard_map/attend/pallas_call | solution.py:334
  88.7 2.0 collective-permute-done.8.got_ref
  95.0 15.0 %collective-permute-done.9.got_ref = bf16[2,4,64,768]{3,2,1,0:T(8,128)(2,1)S(1)} collective-permute-done((bf16[2,4,64,768]{3,2,1,0:T(8,128)(2,1)S(1)}, bf16[2,4,64,768]{3,2,1,0:T(8,128)(2,1)S(1)}, u32[]{:S(2)}, u32[]{:S(2)}) %collective-permute-start.9) | collective-permute-done | bytes 786464 | tf_op jit(solution)/shard_map/ppermute | solution.py:26
  110.8 2.7 %all-gather.2.cloned.1.call-done = bf16[1536,768]{1,0:T(8,128)(2,1)} async-done(((bf16[192,768]{1,0:T(8,128)(2,1)}), bf16[1536,768]{1,0:T(8,128)(2,1)}) %all-gather.2.cloned.1.call-update) | async-done | bytes 2359312 | tf_op jit(solution)/shard_map/all_gather | solution.py:841
  121.7 5.3 %mlp_block.1 = (bf16[1024,768]{1,0:T(8,128)(2,1)S(1)}, bf16[1024,768]{1,0:T(8,128)(2,1)S(1)}, f32[2,4,64,768]{3,2,1,0:T(8,128)S(1)}, bf16[2,4,64,768]{3,2,1,0:T(8,128)(2,1)S(1)}) custom-call(bf16[2,4,64,768]{3,2,1,0:T(8,128)(2,1)S(1)} %get-tuple-element.83.xo_ref, bf16[2,4,64,768]{3,2,1,0:T(8,128)(2,1)S(1)} %collective-permute-done.11.xp_ref, ...), custom_call_target="tpu_custom_call" | custom-call | flops 1400000000 | bytes 1024 | tf_op jit(solution)/shard_map/mlp_block/pallas_call | solution.py:656
  127.4 1.9 collective-permute-done.13.got_ref
  131.5 5.7 %mlp_grads.1 = (bf16[4,2,2,96,768]{4,3,2,1,0:T(8,128)(2,1)S(1)}, f32[2,4,64,768]{3,2,1,0:T(8,128)S(1)}, bf16[2,4,64,768]{3,2,1,0:T(8,128)(2,1)S(1)}, f32[1,768]{1,0:T(1,128)S(1)}) custom-call(bf16[2,4,64,768]{3,2,1,0:T(8,128)(2,1)S(1)} %get-tuple-element.83.xo_ref, bf16[2,4,64,768]{3,2,1,0:T(8,128)(2,1)S(1)} %collective-permute-done.11.xp_ref, ...), custom_call_target="tpu_custom_call" | custom-call | flops 1200000000 | bytes 1024 | tf_op jit(solution)/shard_map/mlp_grads/pallas_call | solution.py:704
  140.7 8.7 %collective-permute-done.14.got_ref = bf16[2,4,64,768]{3,2,1,0:T(8,128)(2,1)} collective-permute-done((bf16[2,4,64,768]{3,2,1,0:T(8,128)(2,1)}, bf16[2,4,64,768]{3,2,1,0:T(8,128)(2,1)}, u32[]{:S(2)}, u32[]{:S(2)}) %collective-permute-start.14) | collective-permute-done | bytes 786464 | tf_op jit(solution)/shard_map/ppermute | solution.py:26
  152.1 2.8 %middle_back.1 = (f32[2,4,64,768]{3,2,1,0:T(8,128)S(1)}, bf16[2,4,64,768]{3,2,1,0:T(8,128)(2,1)S(1)}, f32[4,768]{1,0:T(4,128)S(1)}) custom-call(bf16[2,4,64,768]{3,2,1,0:T(8,128)(2,1)} %add_rows.5.s_ref, bf16[2,4,64,768]{3,2,1,0:T(8,128)(2,1)} %collective-permute-done.14.got_ref, f32[2,4,64,768]{3,2,1,0:T(8,128)S(1)} %copy-done.7, ...), custom_call_target="tpu_custom_call" | custom-call | flops 400000000 | bytes 1024 | tf_op jit(solution)/shard_map/middle_back/pallas_call | solution.py:523
  155.1 2.1 collective-permute-done.15.dp_ref
  158.4 13.9 %attend_back.1 = (bf16[4,4,64,768]{3,2,1,0:T(8,128)(2,1)S(1)}, f32[2,4,64,768]{3,2,1,0:T(8,128)S(1)}, bf16[2,4,64,768]{3,2,1,0:T(8,128)(2,1)S(1)}) custom-call(s32[4]{0:T(128)S(1)} %get-tuple-element.70.lo_ref, s32[4]{0:T(128)S(1)} %get-tuple-element.71.hi_ref, bf16[4,4,64,768]{3,2,1,0:T(8,128)(2,1)S(1)} %copy-done.12, ...), custom_call_target="tpu_custom_call" | custom-call | flops 14000000000 | bytes 1024 | tf_op jit(solution)/shard_map/attend_back/pallas_call | solution.py:455
  175.3 5.5 %attend_grads.1 = (bf16[392,768]{1,0:T(8,128)(2,1)S(1)}, bf16[392,768]{1,0:T(8,128)(2,1)S(1)}, f32[2,768]{1,0:T(2,128)S(1)}) custom-call(s32[1]{0:T(128)} %bitcast.14.flip_ref, f32[1,768]{1,0:T(1,128)S(1)} %get-tuple-element.90.sum_ref, f32[2,768]{1,0:T(2,128)S(1)} %get-tuple-element.171.norm_ref, bf16[1024,768]{1,0:T(8,128)(2,1)S(1)} %bitcast.64, ...), custom_call_target="tpu_custom_call" | custom-call | flops 1200000000 | bytes 1024 | tf_op jit(solution)/shard_map/attend_grads/pallas_call | solution.py:778
  181.1 2.7 %collective-permute-done.20 = f32[6,768]{1,0:T(8,128)S(1)} collective-permute-done((f32[6,768]{1,0:T(8,128)S(1)}, f32[6,768]{1,0:T(8,128)S(1)}, u32[]{:S(2)}, u32[]{:S(2)}) %collective-permute-start.20) | collective-permute-done | bytes 18464 | tf_op jit(solution)/shard_map/ppermute | solution.py:26
  188.0 3.5 %all-to-all-start.1 = ((bf16[4,128,768]{2,1,0:T(8,128)(2,1)}), bf16[4,128,768]{2,1,0:T(8,128)(2,1)S(1)}, u32[]{:S(2)}, u32[]{:S(2)}) async-start(bf16[4,128,768]{2,1,0:T(8,128)(2,1)} %first_back.1), calls=%async_computation.1 | async-start | bytes 1572864 | tf_op jit(solution)/shard_map/all_to_all | solution.py:61
  194.5 6.0 %collective-permute-done.22.got_ref = bf16[392,768]{1,0:T(8,128)(2,1)S(1)} collective-permute-done((bf16[392,768]{1,0:T(8,128)(2,1)S(1)}, bf16[392,768]{1,0:T(8,128)(2,1)S(1)}, u32[]{:S(2)}, u32[]{:S(2)}) %collective-permute-start.22) | collective-permute-done | bytes 602144 | tf_op jit(solution)/shard_map/ppermute | solution.py:26
  203.4 5.6 %collective-permute-done.24 = bf16[2,104,768]{2,1,0:T(8,128)(2,1)S(1)} collective-permute-done((bf16[2,104,768]{2,1,0:T(8,128)(2,1)S(1)}, bf16[2,104,768]{2,1,0:T(8,128)(2,1)S(1)}, u32[]{:S(2)}, u32[]{:S(2)}) %collective-permute-start.24) | collective-permute-done | bytes 319520 | tf_op jit(solution)/shard_map/ppermute | solution.py:26
  209.1 2.2 all-to-all-done.1
  211.4 4.3 %collective-permute-start.30 = (bf16[192,768]{1,0:T(8,128)(2,1)S(1)}, bf16[192,768]{1,0:T(8,128)(2,1)S(1)}, u32[]{:S(2)}, u32[]{:S(2)}) collective-permute-start(bf16[192,768]{1,0:T(8,128)(2,1)S(1)} %bitcast.76), channel_id=1, source_target_pairs={{0,0},{4,1},{8,2},{12,3},{1,4},{5,5},{9,6},{13,7},{2,8},{6,9},{10,... | collective-permute-start | bytes 884744 | tf_op jit(solution)/shard_map/ppermute | solution.py:39
  215.8 1.9 collective-permute-start.25
  217.8 4.6 %collective-permute-start.27 = (bf16[104,768]{1,0:T(8,128)(2,1)S(1)}, bf16[104,768]{1,0:T(8,128)(2,1)S(1)}, u32[]{:S(2)}, u32[]{:S(2)}) collective-permute-start(bf16[104,768]{1,0:T(8,128)(2,1)S(1)} %get-tuple-element.162), channel_id=1, source_target_pairs={{0,2},{1,6},{2,0},{3,4},{4,3},{5,7},{6,1},{7,5},{8,8},{9,12},{10,1... | collective-permute-start | bytes 479240 | tf_op jit(solution)/shard_map/ppermute | solution.py:57
  226.0 5.9 %collective-permute-done.27 = bf16[104,768]{1,0:T(8,128)(2,1)S(1)} collective-permute-done((bf16[104,768]{1,0:T(8,128)(2,1)S(1)}, bf16[104,768]{1,0:T(8,128)(2,1)S(1)}, u32[]{:S(2)}, u32[]{:S(2)}) %collective-permute-start.27) | collective-permute-done | bytes 159776 | tf_op jit(solution)/shard_map/ppermute | solution.py:57
  231.8 11.3 %collective-permute-done.28 = bf16[104,768]{1,0:T(8,128)(2,1)S(1)} collective-permute-done((bf16[104,768]{1,0:T(8,128)(2,1)S(1)}, bf16[104,768]{1,0:T(8,128)(2,1)S(1)}, u32[]{:S(2)}, u32[]{:S(2)}) %collective-permute-start.28) | collective-permute-done | bytes 159776 | tf_op jit(solution)/shard_map/ppermute | solution.py:57
  (185 shorter events, 57.6 us)
Async XLA Ops:
  11.1 15.0 %collective-permute-start = (bf16[104,768]{1,0:T(8,128)(2,1)S(1)}, bf16[104,768]{1,0:T(8,128)(2,1)S(1)}, u32[]{:S(2)}, u32[]{:S(2)}) collective-permute-start(bf16[104,768]{1,0:T(8,128)(2,1)S(1)} %concatenate.35), channel_id=1, source_target_pairs={{0,0},{1,4},{2,8},{3,12},{4,1},{5,5},{6,9},{7,13},{8,2},{9,6},{10,... | collective-permute-start | bytes 479240 | tf_op jit(solution)/shard_map/ppermute | solution.py:34
  15.7 10.5 %collective-permute-start.1 = (bf16[104,768]{1,0:T(8,128)(2,1)S(1)}, bf16[104,768]{1,0:T(8,128)(2,1)S(1)}, u32[]{:S(2)}, u32[]{:S(2)}) collective-permute-start(bf16[104,768]{1,0:T(8,128)(2,1)S(1)} %concatenate.35), channel_id=1, source_target_pairs={{0,1},{1,5},{2,9},{3,13},{4,0},{5,4},{6,8},{7,12},{8,3},{9,7},{10,... | collective-permute-start | bytes 479240 | tf_op jit(solution)/shard_map/ppermute | solution.py:34
  15.8 10.4 %collective-permute-start.2 = (bf16[104,768]{1,0:T(8,128)(2,1)S(1)}, bf16[104,768]{1,0:T(8,128)(2,1)S(1)}, u32[]{:S(2)}, u32[]{:S(2)}) collective-permute-start(bf16[104,768]{1,0:T(8,128)(2,1)S(1)} %concatenate.35), channel_id=1, source_target_pairs={{0,2},{1,6},{2,10},{3,14},{4,3},{5,7},{6,11},{7,15},{8,0},{9,4},{1... | collective-permute-start | bytes 479240 | tf_op jit(solution)/shard_map/ppermute | solution.py:34
  20.8 7.6 %collective-permute-start.3 = (bf16[104,768]{1,0:T(8,128)(2,1)S(1)}, bf16[104,768]{1,0:T(8,128)(2,1)S(1)}, u32[]{:S(2)}, u32[]{:S(2)}) collective-permute-start(bf16[104,768]{1,0:T(8,128)(2,1)S(1)} %concatenate.35), channel_id=1, source_target_pairs={{0,3},{1,7},{2,11},{3,15},{4,2},{5,6},{6,10},{7,14},{8,1},{9,5},{1... | collective-permute-start | bytes 479240 | tf_op jit(solution)/shard_map/ppermute | solution.py:34
  22.5 34.1 %all-to-all-start = ((bf16[4,136,768]{2,1,0:T(8,128)(2,1)}), bf16[4,136,768]{2,1,0:T(8,128)(2,1)S(1)}, u32[]{:S(2)}, u32[]{:S(2)}) async-start(bf16[4,136,768]{2,1,0:T(8,128)(2,1)} %fusion.3), calls=%async_computation | async-start | bytes 1671168 | tf_op jit(solution)/shard_map/all_to_all | solution.py:61
  26.0 87.5 %all-gather.2.cloned.1.call-start = ((), (), s32[]{:S(2)}) async-start(), calls=%async_computation.3 | async-start | bytes 2654208 | tf_op jit(solution)/shard_map/all_gather | solution.py:841
  28.5 23.2 %collective-permute-start.10 = (bf16[192,768]{1,0:T(8,128)(2,1)S(1)}, bf16[192,768]{1,0:T(8,128)(2,1)S(1)}, u32[]{:S(2)}, u32[]{:S(2)}) collective-permute-start(bf16[192,768]{1,0:T(8,128)(2,1)S(1)} %pad_maximum_fusion.4), channel_id=1, source_target_pairs={{0,0},{1,4},{2,8},{3,12},{4,1},{5,5},{6,9},{7,13},{8,2},{9,6},{10,... | collective-permute-start | bytes 884744 | tf_op jit(solution)/shard_map/ppermute | solution.py:34
  46.2 9.1 %collective-permute-start.4 = (bf16[384,768]{1,0:T(8,128)(2,1)S(1)}, bf16[384,768]{1,0:T(8,128)(2,1)S(1)}, u32[]{:S(2)}, u32[]{:S(2)}) collective-permute-start(bf16[384,768]{1,0:T(8,128)(2,1)S(1)} %bitcast.68), channel_id=1, source_target_pairs={{0,16},{16,0},{1,17},{17,1},{2,18},{18,2},{3,19},{19,3},{4,20},{20... | collective-permute-start | bytes 1769480 | tf_op jit(solution)/shard_map/ppermute | solution.py:26
  52.4 149.6 %reduce-scatter.2.cloned.1.call-start = ((), (), s32[]{:S(2)}) async-start(), calls=%async_computation.4 | async-start | bytes 2949120 | tf_op jit(solution)/shard_map/reduce_scatter | solution.py:873
  56.7 8.0 %collective-permute-start.5 = (bf16[1,4,72,768]{3,2,1,0:T(8,128)(2,1)S(1)}, bf16[1,4,72,768]{3,2,1,0:T(8,128)(2,1)S(1)}, u32[]{:S(2)}, u32[]{:S(2)}) collective-permute-start(bf16[1,4,72,768]{3,2,1,0:T(8,128)(2,1)S(1)} %bitcast.69), channel_id=1, source_target_pairs={{0,8},{4,12},{8,0},{12,4},{1,9},{5,13},{9,1},{13,5},{2,10},{6,14},... | collective-permute-start | bytes 1327112 | tf_op jit(solution)/shard_map/ppermute | solution.py:26
  64.8 10.8 %collective-permute-start.6 = (bf16[2,4,72,768]{3,2,1,0:T(8,128)(2,1)S(1)}, bf16[2,4,72,768]{3,2,1,0:T(8,128)(2,1)}, u32[]{:S(2)}, u32[]{:S(2)}) collective-permute-start(bf16[2,4,72,768]{3,2,1,0:T(8,128)(2,1)S(1)} %pad_maximum_fusion.1.xo_ref.x_ref), channel_id=1, source_target_pairs={{0,4},{4,0},{8,12},{12,8},{1,5},{5,1},{9,13},{13,9},{2,6},{6,2},{1... | collective-permute-start | bytes 2654216 | tf_op jit(solution)/shard_map/ppermute | solution.py:26
  73.0 15.3 %collective-permute-start.7 = (bf16[1,4,64,768]{3,2,1,0:T(8,128)(2,1)S(1)}, bf16[1,4,64,768]{3,2,1,0:T(8,128)(2,1)}, u32[]{:S(2)}, u32[]{:S(2)}) collective-permute-start(bf16[1,4,64,768]{3,2,1,0:T(8,128)(2,1)S(1)} %bitcast.71), channel_id=1, source_target_pairs={{0,8},{4,12},{8,0},{12,4},{1,9},{5,13},{9,1},{13,5},{2,10},{6,14},... | collective-permute-start | bytes 1179656 | tf_op jit(solution)/shard_map/ppermute | solution.py:26
  90.9 19.0 %collective-permute-start.9 = (bf16[2,4,64,768]{3,2,1,0:T(8,128)(2,1)S(1)}, bf16[2,4,64,768]{3,2,1,0:T(8,128)(2,1)S(1)}, u32[]{:S(2)}, u32[]{:S(2)}) collective-permute-start(bf16[2,4,64,768]{3,2,1,0:T(8,128)(2,1)S(1)} %add_rows.4.s_ref), channel_id=1, source_target_pairs={{0,8},{4,12},{8,0},{12,4},{1,9},{5,13},{9,1},{13,5},{2,10},{6,14},... | collective-permute-start | bytes 2359304 | tf_op jit(solution)/shard_map/ppermute | solution.py:26
  94.3 25.6 %collective-permute-start.12 = (bf16[2,4,64,768]{3,2,1,0:T(8,128)(2,1)S(1)}, bf16[2,4,64,768]{3,2,1,0:T(8,128)(2,1)}, u32[]{:S(2)}, u32[]{:S(2)}) collective-permute-start(bf16[2,4,64,768]{3,2,1,0:T(8,128)(2,1)S(1)} %pad_maximum_fusion.2.go_ref.g_ref), channel_id=1, source_target_pairs={{0,4},{4,0},{8,12},{12,8},{1,5},{5,1},{9,13},{13,9},{2,6},{6,2},{1... | collective-permute-start | bytes 2359304 | tf_op jit(solution)/shard_map/ppermute | solution.py:26
  117.9 3.8 %collective-permute-start.11 = (bf16[2,4,64,768]{3,2,1,0:T(8,128)(2,1)S(1)}, bf16[2,4,64,768]{3,2,1,0:T(8,128)(2,1)S(1)}, u32[]{:S(2)}, u32[]{:S(2)}) collective-permute-start(bf16[2,4,64,768]{3,2,1,0:T(8,128)(2,1)S(1)} %get-tuple-element.83.xo_ref), channel_id=1, source_target_pairs={{0,4},{4,0},{8,12},{12,8},{1,5},{5,1},{9,13},{13,9},{2,6},{6,2},{1... | collective-permute-start | bytes 2359304 | tf_op jit(solution)/shard_map/ppermute | solution.py:26
  130.4 19.1 %collective-permute-start.14 = (bf16[2,4,64,768]{3,2,1,0:T(8,128)(2,1)}, bf16[2,4,64,768]{3,2,1,0:T(8,128)(2,1)}, u32[]{:S(2)}, u32[]{:S(2)}) collective-permute-start(bf16[2,4,64,768]{3,2,1,0:T(8,128)(2,1)} %add_rows.5.s_ref), channel_id=1, source_target_pairs={{0,8},{4,12},{8,0},{12,4},{1,9},{5,13},{9,1},{13,5},{2,10},{6,14},... | collective-permute-start | bytes 2359304 | tf_op jit(solution)/shard_map/ppermute | solution.py:26
  149.4 5.5 %collective-permute-start.16 = (bf16[2,4,64,768]{3,2,1,0:T(8,128)(2,1)}, bf16[2,4,64,768]{3,2,1,0:T(8,128)(2,1)S(1)}, u32[]{:S(2)}, u32[]{:S(2)}) collective-permute-start(bf16[2,4,64,768]{3,2,1,0:T(8,128)(2,1)} %copy-done.13), channel_id=1, source_target_pairs={{0,4},{4,0},{8,12},{12,8},{1,5},{5,1},{9,13},{13,9},{2,6},{6,2},{1... | collective-permute-start | bytes 2359304 | tf_op jit(solution)/shard_map/ppermute | solution.py:26
  157.2 15.1 %collective-permute-start.17 = (bf16[1,4,64,768]{3,2,1,0:T(8,128)(2,1)S(1)}, bf16[1,4,64,768]{3,2,1,0:T(8,128)(2,1)S(1)}, u32[]{:S(2)}, u32[]{:S(2)}) collective-permute-start(bf16[1,4,64,768]{3,2,1,0:T(8,128)(2,1)S(1)} %get-tuple-element.100), channel_id=1, source_target_pairs={{0,8},{4,12},{8,0},{12,4},{1,9},{5,13},{9,1},{13,5},{2,10},{6,14},... | collective-permute-start | bytes 1179656 | tf_op jit(solution)/shard_map/ppermute | solution.py:26
  172.3 2.4 collective-permute-start.18
  174.9 11.3 %collective-permute-start.19 = (bf16[1,4,64,768]{3,2,1,0:T(8,128)(2,1)S(1)}, bf16[1,4,64,768]{3,2,1,0:T(8,128)(2,1)S(1)}, u32[]{:S(2)}, u32[]{:S(2)}) collective-permute-start(bf16[1,4,64,768]{3,2,1,0:T(8,128)(2,1)S(1)} %get-tuple-element.103), channel_id=1, source_target_pairs={{0,8},{4,12},{8,0},{12,4},{1,9},{5,13},{9,1},{13,5},{2,10},{6,14},... | collective-permute-start | bytes 1179656 | tf_op jit(solution)/shard_map/ppermute | solution.py:26
  180.8 3.0 %collective-permute-start.20 = (f32[6,768]{1,0:T(8,128)S(1)}, f32[6,768]{1,0:T(8,128)S(1)}, u32[]{:S(2)}, u32[]{:S(2)}) collective-permute-start(f32[6,768]{1,0:T(8,128)S(1)} %pad_maximum_fusion.6), channel_id=1, source_target_pairs={{0,16},{16,0},{1,17},{17,1},{2,18},{18,2},{3,19},{19,3},{4,20},{20... | collective-permute-start | bytes 55304 | tf_op jit(solution)/shard_map/ppermute | solution.py:26
  183.8 2.4 collective-permute-start.21
  185.4 15.2 %collective-permute-start.22 = (bf16[392,768]{1,0:T(8,128)(2,1)S(1)}, bf16[392,768]{1,0:T(8,128)(2,1)S(1)}, u32[]{:S(2)}, u32[]{:S(2)}) collective-permute-start(bf16[392,768]{1,0:T(8,128)(2,1)S(1)} %get-tuple-element.112), channel_id=1, source_target_pairs={{0,16},{16,0},{1,17},{17,1},{2,18},{18,2},{3,19},{19,3},{4,20},{20... | collective-permute-start | bytes 1806344 | tf_op jit(solution)/shard_map/ppermute | solution.py:26
  188.0 23.3 %all-to-all-start.1 = ((bf16[4,128,768]{2,1,0:T(8,128)(2,1)}), bf16[4,128,768]{2,1,0:T(8,128)(2,1)S(1)}, u32[]{:S(2)}, u32[]{:S(2)}) async-start(bf16[4,128,768]{2,1,0:T(8,128)(2,1)} %first_back.1), calls=%async_computation.1 | async-start | bytes 1572864 | tf_op jit(solution)/shard_map/all_to_all | solution.py:61
  191.5 3.0 %collective-permute-start.23 = (f32[6,768]{1,0:T(8,128)S(1)}, f32[6,768]{1,0:T(8,128)S(1)}, u32[]{:S(2)}, u32[]{:S(2)}) collective-permute-start(f32[6,768]{1,0:T(8,128)S(1)} %add.65), channel_id=1, source_target_pairs={{0,8},{4,12},{8,0},{12,4},{1,9},{5,13},{9,1},{13,5},{2,10},{6,14},... | collective-permute-start | bytes 55304 | tf_op jit(solution)/shard_map/ppermute | solution.py:26
  200.8 8.3 %collective-permute-start.24 = (bf16[2,104,768]{2,1,0:T(8,128)(2,1)S(1)}, bf16[2,104,768]{2,1,0:T(8,128)(2,1)S(1)}, u32[]{:S(2)}, u32[]{:S(2)}) collective-permute-start(bf16[2,104,768]{2,1,0:T(8,128)(2,1)S(1)} %get-tuple-element.166), channel_id=1, source_target_pairs={{0,8},{4,12},{8,0},{12,4},{1,9},{5,13},{9,1},{13,5},{2,10},{6,14},... | collective-permute-start | bytes 958472 | tf_op jit(solution)/shard_map/ppermute | solution.py:26
  203.1 8.2 %collective-permute-start.29 = (bf16[2,96,768]{2,1,0:T(8,128)(2,1)S(1)}, bf16[2,96,768]{2,1,0:T(8,128)(2,1)S(1)}, u32[]{:S(2)}, u32[]{:S(2)}) collective-permute-start(bf16[2,96,768]{2,1,0:T(8,128)(2,1)S(1)} %dynamic-slice_bitcast_fusion.2), channel_id=1, source_target_pairs={{0,16},{16,0},{1,17},{17,1},{2,18},{18,2},{3,19},{19,3},{4,20},{20... | collective-permute-start | bytes 884744 | tf_op jit(solution)/shard_map/ppermute | solution.py:26
  211.4 31.7 %collective-permute-start.30 = (bf16[192,768]{1,0:T(8,128)(2,1)S(1)}, bf16[192,768]{1,0:T(8,128)(2,1)S(1)}, u32[]{:S(2)}, u32[]{:S(2)}) collective-permute-start(bf16[192,768]{1,0:T(8,128)(2,1)S(1)} %bitcast.76), channel_id=1, source_target_pairs={{0,0},{4,1},{8,2},{12,3},{1,4},{5,5},{9,6},{13,7},{2,8},{6,9},{10,... | collective-permute-start | bytes 884744 | tf_op jit(solution)/shard_map/ppermute | solution.py:39
  215.8 10.2 %collective-permute-start.25 = (bf16[104,768]{1,0:T(8,128)(2,1)S(1)}, bf16[104,768]{1,0:T(8,128)(2,1)S(1)}, u32[]{:S(2)}, u32[]{:S(2)}) collective-permute-start(bf16[104,768]{1,0:T(8,128)(2,1)S(1)} %get-tuple-element.164), channel_id=1, source_target_pairs={{0,0},{1,4},{2,2},{3,6},{4,1},{5,5},{6,3},{7,7},{8,10},{9,14},{10,... | collective-permute-start | bytes 479240 | tf_op jit(solution)/shard_map/ppermute | solution.py:57
  217.7 8.3 %collective-permute-start.26 = (bf16[104,768]{1,0:T(8,128)(2,1)S(1)}, bf16[104,768]{1,0:T(8,128)(2,1)S(1)}, u32[]{:S(2)}, u32[]{:S(2)}) collective-permute-start(bf16[104,768]{1,0:T(8,128)(2,1)S(1)} %get-tuple-element.163), channel_id=1, source_target_pairs={{0,4},{1,0},{2,6},{3,2},{4,5},{5,1},{6,7},{7,3},{8,14},{9,10},{10,... | collective-permute-start | bytes 479240 | tf_op jit(solution)/shard_map/ppermute | solution.py:57
  217.8 14.1 %collective-permute-start.27 = (bf16[104,768]{1,0:T(8,128)(2,1)S(1)}, bf16[104,768]{1,0:T(8,128)(2,1)S(1)}, u32[]{:S(2)}, u32[]{:S(2)}) collective-permute-start(bf16[104,768]{1,0:T(8,128)(2,1)S(1)} %get-tuple-element.162), channel_id=1, source_target_pairs={{0,2},{1,6},{2,0},{3,4},{4,3},{5,7},{6,1},{7,5},{8,8},{9,12},{10,1... | collective-permute-start | bytes 479240 | tf_op jit(solution)/shard_map/ppermute | solution.py:57
  222.3 20.8 %collective-permute-start.28 = (bf16[104,768]{1,0:T(8,128)(2,1)S(1)}, bf16[104,768]{1,0:T(8,128)(2,1)S(1)}, u32[]{:S(2)}, u32[]{:S(2)}) collective-permute-start(bf16[104,768]{1,0:T(8,128)(2,1)S(1)} %get-tuple-element.161), channel_id=1, source_target_pairs={{0,6},{1,2},{2,4},{3,0},{4,7},{5,3},{6,5},{7,1},{8,12},{9,8},{10,1... | collective-permute-start | bytes 479240 | tf_op jit(solution)/shard_map/ppermute | solution.py:57
  (39 other events, 323.6 us)
Sparse Core Ops, SparseCore 0:
  52.5 60.9 all-gather.1
  140.8 45.4 reduce-scatter.1
where the time goes:
time: 260 us; the launch traced here: 255 us
  waiting for transfers between devices  91.9 us (35%)
  starting transfers between devices  72.1 us (28%)
  Pallas kernels  49.9 us (19%)
  local copies, waits for them, and re-layouts  20.8 us (8%)
  between operations  15.3 us (6%)
  other arithmetic  5.25 us (2%)
    ppermute x21, waiting for transfers between devices, xor_swap(): return lax.ppermute(x, axis, [(i, i ^ k) for i in range(n)])  61.1 us
    ppermute x5, starting transfers between devices, send_turned(): return lax.ppermute(x, ('ctx', 'tp'), turn_pairs(lax.axis_size('tp'), k))  27.4 us
    ppermute x21, starting transfers between devices, xor_swap(): return lax.ppermute(x, axis, [(i, i ^ k) for i in range(n)])  25.5 us
    ppermute x4, waiting for transfers between devices, scatter_blocks(): lax.ppermute(pick(four, q ^ k), ('ctx', 'tp'), hop_pairs(n, k))  18.4 us
    unnamed x76, local copies, waits for them, and re-layouts  15.2 us
    pallas_call x1, Pallas kernels, attend_back(): pl.pallas_call(partial(attend_back_kernel, heads), out_shape=(jax.ShapeDt...  13.9 us
    pallas_call x1, Pallas kernels, attend(): pl.pallas_call(partial(attend_kernel, heads), out_shape=(jax.ShapeDtypeSt...  8.92 us
    ppermute x4, starting transfers between devices, scatter_blocks(): lax.ppermute(pick(four, q ^ k), ('ctx', 'tp'), hop_pairs(n, k))  7.86 us
  transfers between devices with their start and end apart: 35, of which 22 were waited for; matrix products, arithmetic and copies ran while one was open for 2% of the time, Pallas kernels for 17%

commit v1 on v0

--- a/solution.py
+++ b/solution.py
@@ -239,11 +239,12 @@
             list_ref[count] = j
 
         count = count + on.astype(jnp.int32)
-    for number in range(1, groups + 1):
-
-        @pl.when(count == number)
+    for number, less in ((2, 0), (groups, 2)):
+
+        @pl.when((count > less) & (count <= number))
         def _():
-            work([list_ref[t] for t in range(number)])
+            js = [list_ref[jnp.minimum(t, count - 1)] for t in range(number)]
+            work(js, count == number)
 
 
 def put_projected(kept_ref, sent_ref, i, project):
@@ -285,11 +286,13 @@
     def per_query(i, carry):
         qs = pl.ds(pl.multiple_of(i * n, n), n)
 
-        def work(js):
+        def work(js, last):
             seg_q = segr_ref[0:1, qs]
+            seg_last = jnp.where(last, seg_q, -1.0)
             q = part_rows(qkv_ref, i, 0) * jnp.asarray(0.125, BF)
             places = [pl.ds(pl.multiple_of(j * n, n), n) for j in js]
-            same = [segc_ref[ks, 0:1] == seg_q for ks in places]
+            same = [segc_ref[ks, 0:1] == seg_q for ks in places[:-1]]
+            same.append(segc_ref[places[-1], 0:1] == seg_last)
             outs = []
             for h in range(heads):
                 qh = only_head(q, h)
@@ -405,16 +408,17 @@
     def per_query(i, carry):
         qs = pl.ds(pl.multiple_of(i * n, n), n)
 
-        def work(js):
+        def work(js, last):
             seg_q = segr_ref[0:1, qs]
+            seg_last = jnp.where(last, seg_q, -1.0)
             q = part_rows(qkv_ref, i, 0) * jnp.asarray(0.125, BF)
             do = do_ref[qs, :]
             qh = [only_head(q, h) for h in range(heads)]
             dh = [only_head(do, h) for h in range(heads)]
             dq = [[] for _ in range(heads)]
-            for j in js:
+            for t, j in enumerate(js):
                 ks = pl.ds(pl.multiple_of(j * n, n), n)
-                same = segc_ref[ks, 0:1] == seg_q
+                same = segc_ref[ks, 0:1] == (seg_q if t < len(js) - 1 else seg_last)
                 dk, dv = [], []
                 for h in range(heads):
                     s = jnp.where(same, nt(kk[ks, :], qh[h]), NEG)
@@ -504,7 +508,8 @@
 
 def middle_back_kernel(s_ref, got_ref, mid_ref, g_ref, vec_ref, dmid_ref, db_ref, sum_ref):
     n = s_ref.shape[0]
-    for i in range(n):
+
+    def step(i, carry):
         dxb = group(s_ref, i).astype(F32) + group(got_ref, n - 1 - i).astype(F32)
         normal, rstd = normed(group(mid_ref, i))
         grad = group(g_ref, i).astype(F32)
@@ -512,11 +517,17 @@
         low = dmid.astype(BF)
         put_rows(dmid_ref, i, dmid)
         put_rows(db_ref, i, low)
-        if i == 0:
+
+        @pl.when(i == 0)
+        def _():
             sum_ref[0:1, :] = jnp.sum(low.astype(F32), 0, keepdims=True)
             sum_ref[1:2, :] = jnp.sum(dxb * normal, 0, keepdims=True)
             sum_ref[2:3, :] = jnp.sum(dxb, 0, keepdims=True)
             sum_ref[3:4, :] = jnp.sum(grad, 0, keepdims=True)
+
+        return carry
+
+    lax.fori_loop(0, n, step, 0)
 
 
 def middle_back(s, got, mid, g, vec):
@@ -694,9 +705,14 @@
 
     lax.fori_loop(0, 2, half_grads, 0)
     size = n // first
-    for i in range(2 * first):
-        result = nt(hidden_ref[i * size : (i + 1) * size, :], weight_part(m_ref, 1))
-        put_rows(kept_ref if i < first else sent_ref, i % first, result)
+    for base, out_ref in ((0, kept_ref), (first, sent_ref)):
+
+        def step(i, carry, base=base, out_ref=out_ref):
+            part = pl.ds(pl.multiple_of((base + i) * size, size), size)
+            put_rows(out_ref, i, nt(hidden_ref[part, :], weight_part(m_ref, 1)))
+            return carry
+
+        lax.fori_loop(0, first, step, 0)
     sum_ref[...] = jnp.sum(dpre_ref[...].astype(F32), 0, keepdims=True)
 
 
@@ -739,18 +755,20 @@
     half = width // 2
     n = do_ref.shape[0]
     block = rows // (2 * first)
-    gain = bias = jnp.zeros((1, width), F32)
-    for i in range(2 * first):
-        x_ref, g_ref = (xo_ref, kept_ref) if i < first else (xp_ref, sent_ref)
-        normal, _ = normed(x_rows(x_ref, i % first, thin).astype(F32))
-        xa[i * block : (i + 1) * block, :] = (
-            normal * norm_ref[0:1, :] + norm_ref[1:2, :]
-        ).astype(BF)
-        dx = group(g_ref, i % first).astype(F32)
-        gain = gain + jnp.sum(dx * normal, 0, keepdims=True)
-        bias = bias + jnp.sum(dx, 0, keepdims=True)
-    vec_ref[0:1, :] = gain
-    vec_ref[1:2, :] = bias
+    vec_ref[...] = jnp.zeros_like(vec_ref)
+    for base, x_ref, g_ref in ((0, xo_ref, kept_ref), (first, xp_ref, sent_ref)):
+
+        def step(i, carry, base=base, x_ref=x_ref, g_ref=g_ref):
+            normal, _ = normed(x_rows(x_ref, i, thin).astype(F32))
+            xa[pl.ds(pl.multiple_of((base + i) * block, block), block), :] = (
+                normal * norm_ref[0:1, :] + norm_ref[1:2, :]
+            ).astype(BF)
+            dx = group(g_ref, i).astype(F32)
+            vec_ref[0:1, :] += jnp.sum(dx * normal, 0, keepdims=True)
+            vec_ref[1:2, :] += jnp.sum(dx, 0, keepdims=True)
+            return carry
+
+        lax.fori_loop(0, first, step, 0)
     totals = [
         jnp.sum(dmix_ref[:, lanes_of(dmix_ref, c)].astype(F32), 0, keepdims=True).astype(BF)
         for c in (0, 2)

time: 260 us -> 256 us (0.985); the launches traced: 255 us -> 256 us
  transfers between devices with their start and end apart: 35 -> 35, of which waited for: 22 -> 22; matrix products, arithmetic and copies ran while one was open for 2% -> 2% of each run, Pallas kernels for 17% -> 18%
where the time goes in v1:
time: 256 us
  waiting for transfers between devices  90.2 us (35%)
  starting transfers between devices  72.5 us (28%)
  Pallas kernels  52 us (20%)
  local copies, waits for them, and re-layouts  20.8 us (8%)
  between operations  14.8 us (6%)
  other arithmetic  5.26 us (2%)
    ppermute x21, waiting for transfers between devices, xor_swap(): return lax.ppermute(x, axis, [(i, i ^ k) for i in range(n)])  60.4 us
    ppermute x5, starting transfers between devices, send_turned(): return lax.ppermute(x, ('ctx', 'tp'), turn_pairs(lax.axis_size('tp'), k))  27.4 us
    ppermute x21, starting transfers between devices, xor_swap(): return lax.ppermute(x, axis, [(i, i ^ k) for i in range(n)])  25.6 us
    ppermute x4, waiting for transfers between devices, scatter_blocks(): lax.ppermute(pick(four, q ^ k), ('ctx', 'tp'), hop_pairs(n, k))  18.4 us
    unnamed x76, local copies, waits for them, and re-layouts  15.2 us
    pallas_call x1, Pallas kernels, attend_back(): pl.pallas_call(partial(attend_back_kernel, heads), out_shape=(jax.ShapeDt...  14.9 us
    pallas_call x1, Pallas kernels, attend(): pl.pallas_call(partial(attend_kernel, heads), out_shape=(jax.ShapeDtypeSt...  9.61 us
    ppermute x4, starting transfers between devices, scatter_blocks(): lax.ppermute(pick(four, q ^ k), ('ctx', 'tp'), hop_pairs(n, k))  7.86 us
  transfers between devices with their start and end apart: 35, of which 22 were waited for; matrix products, arithmetic and copies ran while one was open for 2% of the time, Pallas kernels for 18%

profile of v1, /device:TPU:1, one launch (start us, length us, event | category | flops | bytes accessed | tf_op | source)
XLA Modules:
  0.0 255.6 jit_solution(7601286584719002604)
XLA Ops:
  11.1 4.6 %collective-permute-start = (bf16[104,768]{1,0:T(8,128)(2,1)S(1)}, bf16[104,768]{1,0:T(8,128)(2,1)S(1)}, u32[]{:S(2)}, u32[]{:S(2)}) collective-permute-start(bf16[104,768]{1,0:T(8,128)(2,1)S(1)} %concatenate.35), channel_id=1, source_target_pairs={{0,0},{1,4},{2,8},{3,12},{4,1},{5,5},{6,9},{7,13},{8,2},{9,6},{10,... | collective-permute-start | bytes 479240 | tf_op jit(solution)/shard_map/ppermute | solution.py:34
  15.8 5.0 %collective-permute-start.2 = (bf16[104,768]{1,0:T(8,128)(2,1)S(1)}, bf16[104,768]{1,0:T(8,128)(2,1)S(1)}, u32[]{:S(2)}, u32[]{:S(2)}) collective-permute-start(bf16[104,768]{1,0:T(8,128)(2,1)S(1)} %concatenate.35), channel_id=1, source_target_pairs={{0,2},{1,6},{2,10},{3,14},{4,3},{5,7},{6,11},{7,15},{8,0},{9,4},{1... | collective-permute-start | bytes 479240 | tf_op jit(solution)/shard_map/ppermute | solution.py:34
  22.5 3.5 %all-to-all-start = ((bf16[4,136,768]{2,1,0:T(8,128)(2,1)}), bf16[4,136,768]{2,1,0:T(8,128)(2,1)S(1)}, u32[]{:S(2)}, u32[]{:S(2)}) async-start(bf16[4,136,768]{2,1,0:T(8,128)(2,1)} %fusion.3), calls=%async_computation | async-start | bytes 1671168 | tf_op jit(solution)/shard_map/all_to_all | solution.py:61
  26.3 2.2 collective-permute-done.3
  28.5 17.8 %collective-permute-start.10 = (bf16[192,768]{1,0:T(8,128)(2,1)S(1)}, bf16[192,768]{1,0:T(8,128)(2,1)S(1)}, u32[]{:S(2)}, u32[]{:S(2)}) collective-permute-start(bf16[192,768]{1,0:T(8,128)(2,1)S(1)} %pad_maximum_fusion.4), channel_id=1, source_target_pairs={{0,0},{1,4},{2,8},{3,12},{4,1},{5,5},{6,9},{7,13},{8,2},{9,6},{10,... | collective-permute-start | bytes 884744 | tf_op jit(solution)/shard_map/ppermute | solution.py:34
  47.5 4.2 %collective-permute-done.10 = bf16[192,768]{1,0:T(8,128)(2,1)S(1)} collective-permute-done((bf16[192,768]{1,0:T(8,128)(2,1)S(1)}, bf16[192,768]{1,0:T(8,128)(2,1)S(1)}, u32[]{:S(2)}, u32[]{:S(2)}) %collective-permute-start.10) | collective-permute-done | bytes 294944 | tf_op jit(solution)/shard_map/ppermute | solution.py:34
  52.5 2.9 %collective-permute-done.4 = bf16[384,768]{1,0:T(8,128)(2,1)S(1)} collective-permute-done((bf16[384,768]{1,0:T(8,128)(2,1)S(1)}, bf16[384,768]{1,0:T(8,128)(2,1)S(1)}, u32[]{:S(2)}, u32[]{:S(2)}) %collective-permute-start.4) | collective-permute-done | bytes 589856 | tf_op jit(solution)/shard_map/ppermute | solution.py:26
  56.8 7.9 %collective-permute-done.5 = bf16[1,4,72,768]{3,2,1,0:T(8,128)(2,1)S(1)} collective-permute-done((bf16[1,4,72,768]{3,2,1,0:T(8,128)(2,1)S(1)}, bf16[1,4,72,768]{3,2,1,0:T(8,128)(2,1)S(1)}, u32[]{:S(2)}, u32[]{:S(2)}) %collective-permute-start.5) | collective-permute-done | bytes 442400 | tf_op jit(solution)/shard_map/ppermute | solution.py:26
  64.8 8.2 %collective-permute-start.6 = (bf16[2,4,72,768]{3,2,1,0:T(8,128)(2,1)S(1)}, bf16[2,4,72,768]{3,2,1,0:T(8,128)(2,1)}, u32[]{:S(2)}, u32[]{:S(2)}) collective-permute-start(bf16[2,4,72,768]{3,2,1,0:T(8,128)(2,1)S(1)} %pad_maximum_fusion.1.xo_ref.x_ref), channel_id=1, source_target_pairs={{0,4},{4,0},{8,12},{12,8},{1,5},{5,1},{9,13},{13,9},{2,6},{6,2},{1... | collective-permute-start | bytes 2654216 | tf_op jit(solution)/shard_map/ppermute | solution.py:26
  75.6 3.7 %qkv.1 = (bf16[4,4,64,768]{3,2,1,0:T(8,128)(2,1)S(1)}, f32[8,1024]{1,0:T(8,128)S(1)}, s32[4]{0:T(128)S(1)}, s32[4]{0:T(128)S(1)}) custom-call(bf16[2,4,72,768]{3,2,1,0:T(8,128)(2,1)S(1)} %pad_maximum_fusion.1.xo_ref.x_ref, bf16[2,4,72,768]{3,2,1,0:T(8,128)(2,1)} %collective-permute-done.6.xp_ref, f32[6,768]{1,0:T(8,128)S(1)} %stack.43.vec_ref, ...), custom_call_target="tpu_custom_call" | custom-call | flops 800000000 | bytes 1024 | tf_op jit(solution)/shard_map/qkv/pallas_call | solution.py:174
  79.3 9.6 %attend.1 = (bf16[4,4,64,192]{3,2,1,0:T(8,128)(2,1)S(1)}, f32[8,1024]{1,0:T(8,128)S(1)}, f32[2,4,64,768]{3,2,1,0:T(8,128)S(1)}, bf16[2,4,64,768]{3,2,1,0:T(8,128)(2,1)S(1)}) custom-call(s32[4]{0:T(128)S(1)} %get-tuple-element.70.lo_ref, s32[4]{0:T(128)S(1)} %get-tuple-element.71.hi_ref, bf16[4,4,64,768]{3,2,1,0:T(8,128)(2,1)S(1)} %get-tuple-element.72.qkv_ref, ...), custom_call_target="tpu_custom_call" | custom-call | flops 2200000000 | bytes 1024 | tf_op jit(solution)/shard_map/attend/pallas_call | solution.py:337
  89.4 2.0 collective-permute-done.8.got_ref
  95.7 14.9 %collective-permute-done.9.got_ref = bf16[2,4,64,768]{3,2,1,0:T(8,128)(2,1)S(1)} collective-permute-done((bf16[2,4,64,768]{3,2,1,0:T(8,128)(2,1)S(1)}, bf16[2,4,64,768]{3,2,1,0:T(8,128)(2,1)S(1)}, u32[]{:S(2)}, u32[]{:S(2)}) %collective-permute-start.9) | collective-permute-done | bytes 786464 | tf_op jit(solution)/shard_map/ppermute | solution.py:26
  111.5 2.0 all-gather.2.cloned.1.call-done
  121.7 5.3 %mlp_block.1 = (bf16[1024,768]{1,0:T(8,128)(2,1)S(1)}, bf16[1024,768]{1,0:T(8,128)(2,1)S(1)}, f32[2,4,64,768]{3,2,1,0:T(8,128)S(1)}, bf16[2,4,64,768]{3,2,1,0:T(8,128)(2,1)S(1)}) custom-call(bf16[2,4,64,768]{3,2,1,0:T(8,128)(2,1)S(1)} %get-tuple-element.83.xo_ref, bf16[2,4,64,768]{3,2,1,0:T(8,128)(2,1)S(1)} %collective-permute-done.11.xp_ref, ...), custom_call_target="tpu_custom_call" | custom-call | flops 1400000000 | bytes 1024 | tf_op jit(solution)/shard_map/mlp_block/pallas_call | solution.py:667
  127.4 1.9 collective-permute-done.13.got_ref
  131.5 6.3 %mlp_grads.1 = (bf16[4,2,2,96,768]{4,3,2,1,0:T(8,128)(2,1)S(1)}, f32[2,4,64,768]{3,2,1,0:T(8,128)S(1)}, bf16[2,4,64,768]{3,2,1,0:T(8,128)(2,1)S(1)}, f32[1,768]{1,0:T(1,128)S(1)}) custom-call(bf16[2,4,64,768]{3,2,1,0:T(8,128)(2,1)S(1)} %get-tuple-element.83.xo_ref, bf16[2,4,64,768]{3,2,1,0:T(8,128)(2,1)S(1)} %collective-permute-done.11.xp_ref, ...), custom_call_target="tpu_custom_call" | custom-call | flops 1200000000 | bytes 1024 | tf_op jit(solution)/shard_map/mlp_grads/pallas_call | solution.py:720
  141.3 8.1 %collective-permute-done.14.got_ref = bf16[2,4,64,768]{3,2,1,0:T(8,128)(2,1)} collective-permute-done((bf16[2,4,64,768]{3,2,1,0:T(8,128)(2,1)}, bf16[2,4,64,768]{3,2,1,0:T(8,128)(2,1)}, u32[]{:S(2)}, u32[]{:S(2)}) %collective-permute-start.14) | collective-permute-done | bytes 786464 | tf_op jit(solution)/shard_map/ppermute | solution.py:26
  152.0 3.2 %middle_back.1 = (f32[2,4,64,768]{3,2,1,0:T(8,128)S(1)}, bf16[2,4,64,768]{3,2,1,0:T(8,128)(2,1)S(1)}, f32[4,768]{1,0:T(4,128)S(1)}) custom-call(bf16[2,4,64,768]{3,2,1,0:T(8,128)(2,1)} %add_rows.5.s_ref, bf16[2,4,64,768]{3,2,1,0:T(8,128)(2,1)} %collective-permute-done.14.got_ref, f32[2,4,64,768]{3,2,1,0:T(8,128)S(1)} %copy-done.7, ...), custom_call_target="tpu_custom_call" | custom-call | flops 400000000 | bytes 1024 | tf_op jit(solution)/shard_map/middle_back/pallas_call | solution.py:534
  155.4 2.1 collective-permute-done.15.dp_ref
  158.8 14.9 %attend_back.1 = (bf16[4,4,64,768]{3,2,1,0:T(8,128)(2,1)S(1)}, f32[2,4,64,768]{3,2,1,0:T(8,128)S(1)}, bf16[2,4,64,768]{3,2,1,0:T(8,128)(2,1)S(1)}) custom-call(s32[4]{0:T(128)S(1)} %get-tuple-element.70.lo_ref, s32[4]{0:T(128)S(1)} %get-tuple-element.71.hi_ref, bf16[4,4,64,768]{3,2,1,0:T(8,128)(2,1)S(1)} %copy-done.12, ...), custom_call_target="tpu_custom_call" | custom-call | flops 14000000000 | bytes 1024 | tf_op jit(solution)/shard_map/attend_back/pallas_call | solution.py:459
  176.5 5.0 %attend_grads.1 = (bf16[392,768]{1,0:T(8,128)(2,1)S(1)}, bf16[392,768]{1,0:T(8,128)(2,1)S(1)}, f32[2,768]{1,0:T(2,128)S(1)}) custom-call(s32[1]{0:T(128)} %bitcast.14.flip_ref, f32[1,768]{1,0:T(1,128)S(1)} %get-tuple-element.90.sum_ref, f32[2,768]{1,0:T(2,128)S(1)} %get-tuple-element.171.norm_ref, bf16[1024,768]{1,0:T(8,128)(2,1)S(1)} %bitcast.64, ...), custom_call_target="tpu_custom_call" | custom-call | flops 1200000000 | bytes 1024 | tf_op jit(solution)/shard_map/attend_grads/pallas_call | solution.py:796
  181.9 2.7 %collective-permute-done.20 = f32[6,768]{1,0:T(8,128)S(1)} collective-permute-done((f32[6,768]{1,0:T(8,128)S(1)}, f32[6,768]{1,0:T(8,128)S(1)}, u32[]{:S(2)}, u32[]{:S(2)}) %collective-permute-start.20) | collective-permute-done | bytes 18464 | tf_op jit(solution)/shard_map/ppermute | solution.py:26
  188.8 3.5 %all-to-all-start.1 = ((bf16[4,128,768]{2,1,0:T(8,128)(2,1)}), bf16[4,128,768]{2,1,0:T(8,128)(2,1)S(1)}, u32[]{:S(2)}, u32[]{:S(2)}) async-start(bf16[4,128,768]{2,1,0:T(8,128)(2,1)} %first_back.1), calls=%async_computation.1 | async-start | bytes 1572864 | tf_op jit(solution)/shard_map/all_to_all | solution.py:61
  195.3 6.0 %collective-permute-done.22.got_ref = bf16[392,768]{1,0:T(8,128)(2,1)S(1)} collective-permute-done((bf16[392,768]{1,0:T(8,128)(2,1)S(1)}, bf16[392,768]{1,0:T(8,128)(2,1)S(1)}, u32[]{:S(2)}, u32[]{:S(2)}) %collective-permute-start.22) | collective-permute-done | bytes 602144 | tf_op jit(solution)/shard_map/ppermute | solution.py:26
  204.2 5.6 %collective-permute-done.24 = bf16[2,104,768]{2,1,0:T(8,128)(2,1)S(1)} collective-permute-done((bf16[2,104,768]{2,1,0:T(8,128)(2,1)S(1)}, bf16[2,104,768]{2,1,0:T(8,128)(2,1)S(1)}, u32[]{:S(2)}, u32[]{:S(2)}) %collective-permute-start.24) | collective-permute-done | bytes 319520 | tf_op jit(solution)/shard_map/ppermute | solution.py:26
  209.9 2.0 all-to-all-done.1
  211.9 4.5 %collective-permute-start.30 = (bf16[192,768]{1,0:T(8,128)(2,1)S(1)}, bf16[192,768]{1,0:T(8,128)(2,1)S(1)}, u32[]{:S(2)}, u32[]{:S(2)}) collective-permute-start(bf16[192,768]{1,0:T(8,128)(2,1)S(1)} %bitcast.76), channel_id=1, source_target_pairs={{0,0},{4,1},{8,2},{12,3},{1,4},{5,5},{9,6},{13,7},{2,8},{6,9},{10,... | collective-permute-start | bytes 884744 | tf_op jit(solution)/shard_map/ppermute | solution.py:39
  216.5 1.9 collective-permute-start.25
  218.5 4.5 %collective-permute-start.27 = (bf16[104,768]{1,0:T(8,128)(2,1)S(1)}, bf16[104,768]{1,0:T(8,128)(2,1)S(1)}, u32[]{:S(2)}, u32[]{:S(2)}) collective-permute-start(bf16[104,768]{1,0:T(8,128)(2,1)S(1)} %get-tuple-element.162), channel_id=1, source_target_pairs={{0,2},{1,6},{2,0},{3,4},{4,3},{5,7},{6,1},{7,5},{8,8},{9,12},{10,1... | collective-permute-start | bytes 479240 | tf_op jit(solution)/shard_map/ppermute | solution.py:57
  226.8 5.8 %collective-permute-done.27 = bf16[104,768]{1,0:T(8,128)(2,1)S(1)} collective-permute-done((bf16[104,768]{1,0:T(8,128)(2,1)S(1)}, bf16[104,768]{1,0:T(8,128)(2,1)S(1)}, u32[]{:S(2)}, u32[]{:S(2)}) %collective-permute-start.27) | collective-permute-done | bytes 159776 | tf_op jit(solution)/shard_map/ppermute | solution.py:57
  232.6 11.3 %collective-permute-done.28 = bf16[104,768]{1,0:T(8,128)(2,1)S(1)} collective-permute-done((bf16[104,768]{1,0:T(8,128)(2,1)S(1)}, bf16[104,768]{1,0:T(8,128)(2,1)S(1)}, u32[]{:S(2)}, u32[]{:S(2)}) %collective-permute-start.28) | collective-permute-done | bytes 159776 | tf_op jit(solution)/shard_map/ppermute | solution.py:57
  (185 shorter events, 57.7 us)
Async XLA Ops:
  11.1 15.0 %collective-permute-start = (bf16[104,768]{1,0:T(8,128)(2,1)S(1)}, bf16[104,768]{1,0:T(8,128)(2,1)S(1)}, u32[]{:S(2)}, u32[]{:S(2)}) collective-permute-start(bf16[104,768]{1,0:T(8,128)(2,1)S(1)} %concatenate.35), channel_id=1, source_target_pairs={{0,0},{1,4},{2,8},{3,12},{4,1},{5,5},{6,9},{7,13},{8,2},{9,6},{10,... | collective-permute-start | bytes 479240 | tf_op jit(solution)/shard_map/ppermute | solution.py:34
  15.7 10.5 %collective-permute-start.1 = (bf16[104,768]{1,0:T(8,128)(2,1)S(1)}, bf16[104,768]{1,0:T(8,128)(2,1)S(1)}, u32[]{:S(2)}, u32[]{:S(2)}) collective-permute-start(bf16[104,768]{1,0:T(8,128)(2,1)S(1)} %concatenate.35), channel_id=1, source_target_pairs={{0,1},{1,5},{2,9},{3,13},{4,0},{5,4},{6,8},{7,12},{8,3},{9,7},{10,... | collective-permute-start | bytes 479240 | tf_op jit(solution)/shard_map/ppermute | solution.py:34
  15.8 10.4 %collective-permute-start.2 = (bf16[104,768]{1,0:T(8,128)(2,1)S(1)}, bf16[104,768]{1,0:T(8,128)(2,1)S(1)}, u32[]{:S(2)}, u32[]{:S(2)}) collective-permute-start(bf16[104,768]{1,0:T(8,128)(2,1)S(1)} %concatenate.35), channel_id=1, source_target_pairs={{0,2},{1,6},{2,10},{3,14},{4,3},{5,7},{6,11},{7,15},{8,0},{9,4},{1... | collective-permute-start | bytes 479240 | tf_op jit(solution)/shard_map/ppermute | solution.py:34
  20.8 7.6 %collective-permute-start.3 = (bf16[104,768]{1,0:T(8,128)(2,1)S(1)}, bf16[104,768]{1,0:T(8,128)(2,1)S(1)}, u32[]{:S(2)}, u32[]{:S(2)}) collective-permute-start(bf16[104,768]{1,0:T(8,128)(2,1)S(1)} %concatenate.35), channel_id=1, source_target_pairs={{0,3},{1,7},{2,11},{3,15},{4,2},{5,6},{6,10},{7,14},{8,1},{9,5},{1... | collective-permute-start | bytes 479240 | tf_op jit(solution)/shard_map/ppermute | solution.py:34
  22.5 34.1 %all-to-all-start = ((bf16[4,136,768]{2,1,0:T(8,128)(2,1)}), bf16[4,136,768]{2,1,0:T(8,128)(2,1)S(1)}, u32[]{:S(2)}, u32[]{:S(2)}) async-start(bf16[4,136,768]{2,1,0:T(8,128)(2,1)} %fusion.3), calls=%async_computation | async-start | bytes 1671168 | tf_op jit(solution)/shard_map/all_to_all | solution.py:61
  26.0 87.5 %all-gather.2.cloned.1.call-start = ((), (), s32[]{:S(2)}) async-start(), calls=%async_computation.3 | async-start | bytes 2654208 | tf_op jit(solution)/shard_map/all_gather | solution.py:859
  28.5 23.2 %collective-permute-start.10 = (bf16[192,768]{1,0:T(8,128)(2,1)S(1)}, bf16[192,768]{1,0:T(8,128)(2,1)S(1)}, u32[]{:S(2)}, u32[]{:S(2)}) collective-permute-start(bf16[192,768]{1,0:T(8,128)(2,1)S(1)} %pad_maximum_fusion.4), channel_id=1, source_target_pairs={{0,0},{1,4},{2,8},{3,12},{4,1},{5,5},{6,9},{7,13},{8,2},{9,6},{10,... | collective-permute-start | bytes 884744 | tf_op jit(solution)/shard_map/ppermute | solution.py:34
  46.2 9.1 %collective-permute-start.4 = (bf16[384,768]{1,0:T(8,128)(2,1)S(1)}, bf16[384,768]{1,0:T(8,128)(2,1)S(1)}, u32[]{:S(2)}, u32[]{:S(2)}) collective-permute-start(bf16[384,768]{1,0:T(8,128)(2,1)S(1)} %bitcast.68), channel_id=1, source_target_pairs={{0,16},{16,0},{1,17},{17,1},{2,18},{18,2},{3,19},{19,3},{4,20},{20... | collective-permute-start | bytes 1769480 | tf_op jit(solution)/shard_map/ppermute | solution.py:26
  52.4 150.4 %reduce-scatter.2.cloned.1.call-start = ((), (), s32[]{:S(2)}) async-start(), calls=%async_computation.4 | async-start | bytes 2949120 | tf_op jit(solution)/shard_map/reduce_scatter | solution.py:891
  56.7 8.0 %collective-permute-start.5 = (bf16[1,4,72,768]{3,2,1,0:T(8,128)(2,1)S(1)}, bf16[1,4,72,768]{3,2,1,0:T(8,128)(2,1)S(1)}, u32[]{:S(2)}, u32[]{:S(2)}) collective-permute-start(bf16[1,4,72,768]{3,2,1,0:T(8,128)(2,1)S(1)} %bitcast.69), channel_id=1, source_target_pairs={{0,8},{4,12},{8,0},{12,4},{1,9},{5,13},{9,1},{13,5},{2,10},{6,14},... | collective-permute-start | bytes 1327112 | tf_op jit(solution)/shard_map/ppermute | solution.py:26
  64.8 10.8 %collective-permute-start.6 = (bf16[2,4,72,768]{3,2,1,0:T(8,128)(2,1)S(1)}, bf16[2,4,72,768]{3,2,1,0:T(8,128)(2,1)}, u32[]{:S(2)}, u32[]{:S(2)}) collective-permute-start(bf16[2,4,72,768]{3,2,1,0:T(8,128)(2,1)S(1)} %pad_maximum_fusion.1.xo_ref.x_ref), channel_id=1, source_target_pairs={{0,4},{4,0},{8,12},{12,8},{1,5},{5,1},{9,13},{13,9},{2,6},{6,2},{1... | collective-permute-start | bytes 2654216 | tf_op jit(solution)/shard_map/ppermute | solution.py:26
  73.0 16.0 %collective-permute-start.7 = (bf16[1,4,64,768]{3,2,1,0:T(8,128)(2,1)S(1)}, bf16[1,4,64,768]{3,2,1,0:T(8,128)(2,1)}, u32[]{:S(2)}, u32[]{:S(2)}) collective-permute-start(bf16[1,4,64,768]{3,2,1,0:T(8,128)(2,1)S(1)} %bitcast.71), channel_id=1, source_target_pairs={{0,8},{4,12},{8,0},{12,4},{1,9},{5,13},{9,1},{13,5},{2,10},{6,14},... | collective-permute-start | bytes 1179656 | tf_op jit(solution)/shard_map/ppermute | solution.py:26
  91.6 19.0 %collective-permute-start.9 = (bf16[2,4,64,768]{3,2,1,0:T(8,128)(2,1)S(1)}, bf16[2,4,64,768]{3,2,1,0:T(8,128)(2,1)S(1)}, u32[]{:S(2)}, u32[]{:S(2)}) collective-permute-start(bf16[2,4,64,768]{3,2,1,0:T(8,128)(2,1)S(1)} %add_rows.4.s_ref), channel_id=1, source_target_pairs={{0,8},{4,12},{8,0},{12,4},{1,9},{5,13},{9,1},{13,5},{2,10},{6,14},... | collective-permute-start | bytes 2359304 | tf_op jit(solution)/shard_map/ppermute | solution.py:26
  94.9 24.9 %collective-permute-start.12 = (bf16[2,4,64,768]{3,2,1,0:T(8,128)(2,1)S(1)}, bf16[2,4,64,768]{3,2,1,0:T(8,128)(2,1)}, u32[]{:S(2)}, u32[]{:S(2)}) collective-permute-start(bf16[2,4,64,768]{3,2,1,0:T(8,128)(2,1)S(1)} %pad_maximum_fusion.2.go_ref.g_ref), channel_id=1, source_target_pairs={{0,4},{4,0},{8,12},{12,8},{1,5},{5,1},{9,13},{13,9},{2,6},{6,2},{1... | collective-permute-start | bytes 2359304 | tf_op jit(solution)/shard_map/ppermute | solution.py:26
  117.9 3.8 %collective-permute-start.11 = (bf16[2,4,64,768]{3,2,1,0:T(8,128)(2,1)S(1)}, bf16[2,4,64,768]{3,2,1,0:T(8,128)(2,1)S(1)}, u32[]{:S(2)}, u32[]{:S(2)}) collective-permute-start(bf16[2,4,64,768]{3,2,1,0:T(8,128)(2,1)S(1)} %get-tuple-element.83.xo_ref), channel_id=1, source_target_pairs={{0,4},{4,0},{8,12},{12,8},{1,5},{5,1},{9,13},{13,9},{2,6},{6,2},{1... | collective-permute-start | bytes 2359304 | tf_op jit(solution)/shard_map/ppermute | solution.py:26
  130.3 19.1 %collective-permute-start.14 = (bf16[2,4,64,768]{3,2,1,0:T(8,128)(2,1)}, bf16[2,4,64,768]{3,2,1,0:T(8,128)(2,1)}, u32[]{:S(2)}, u32[]{:S(2)}) collective-permute-start(bf16[2,4,64,768]{3,2,1,0:T(8,128)(2,1)} %add_rows.5.s_ref), channel_id=1, source_target_pairs={{0,8},{4,12},{8,0},{12,4},{1,9},{5,13},{9,1},{13,5},{2,10},{6,14},... | collective-permute-start | bytes 2359304 | tf_op jit(solution)/shard_map/ppermute | solution.py:26
  149.4 5.9 %collective-permute-start.16 = (bf16[2,4,64,768]{3,2,1,0:T(8,128)(2,1)}, bf16[2,4,64,768]{3,2,1,0:T(8,128)(2,1)S(1)}, u32[]{:S(2)}, u32[]{:S(2)}) collective-permute-start(bf16[2,4,64,768]{3,2,1,0:T(8,128)(2,1)} %copy-done.13), channel_id=1, source_target_pairs={{0,4},{4,0},{8,12},{12,8},{1,5},{5,1},{9,13},{13,9},{2,6},{6,2},{1... | collective-permute-start | bytes 2359304 | tf_op jit(solution)/shard_map/ppermute | solution.py:26
  157.5 16.1 %collective-permute-start.17 = (bf16[1,4,64,768]{3,2,1,0:T(8,128)(2,1)S(1)}, bf16[1,4,64,768]{3,2,1,0:T(8,128)(2,1)S(1)}, u32[]{:S(2)}, u32[]{:S(2)}) collective-permute-start(bf16[1,4,64,768]{3,2,1,0:T(8,128)(2,1)S(1)} %get-tuple-element.100), channel_id=1, source_target_pairs={{0,8},{4,12},{8,0},{12,4},{1,9},{5,13},{9,1},{13,5},{2,10},{6,14},... | collective-permute-start | bytes 1179656 | tf_op jit(solution)/shard_map/ppermute | solution.py:26
  173.6 2.4 collective-permute-start.18
  176.2 10.8 %collective-permute-start.19 = (bf16[1,4,64,768]{3,2,1,0:T(8,128)(2,1)S(1)}, bf16[1,4,64,768]{3,2,1,0:T(8,128)(2,1)S(1)}, u32[]{:S(2)}, u32[]{:S(2)}) collective-permute-start(bf16[1,4,64,768]{3,2,1,0:T(8,128)(2,1)S(1)} %get-tuple-element.103), channel_id=1, source_target_pairs={{0,8},{4,12},{8,0},{12,4},{1,9},{5,13},{9,1},{13,5},{2,10},{6,14},... | collective-permute-start | bytes 1179656 | tf_op jit(solution)/shard_map/ppermute | solution.py:26
  181.5 3.0 %collective-permute-start.20 = (f32[6,768]{1,0:T(8,128)S(1)}, f32[6,768]{1,0:T(8,128)S(1)}, u32[]{:S(2)}, u32[]{:S(2)}) collective-permute-start(f32[6,768]{1,0:T(8,128)S(1)} %pad_maximum_fusion.6), channel_id=1, source_target_pairs={{0,16},{16,0},{1,17},{17,1},{2,18},{18,2},{3,19},{19,3},{4,20},{20... | collective-permute-start | bytes 55304 | tf_op jit(solution)/shard_map/ppermute | solution.py:26
  184.6 2.4 collective-permute-start.21
  186.2 15.2 %collective-permute-start.22 = (bf16[392,768]{1,0:T(8,128)(2,1)S(1)}, bf16[392,768]{1,0:T(8,128)(2,1)S(1)}, u32[]{:S(2)}, u32[]{:S(2)}) collective-permute-start(bf16[392,768]{1,0:T(8,128)(2,1)S(1)} %get-tuple-element.112), channel_id=1, source_target_pairs={{0,16},{16,0},{1,17},{17,1},{2,18},{18,2},{3,19},{19,3},{4,20},{20... | collective-permute-start | bytes 1806344 | tf_op jit(solution)/shard_map/ppermute | solution.py:26
  188.8 23.1 %all-to-all-start.1 = ((bf16[4,128,768]{2,1,0:T(8,128)(2,1)}), bf16[4,128,768]{2,1,0:T(8,128)(2,1)S(1)}, u32[]{:S(2)}, u32[]{:S(2)}) async-start(bf16[4,128,768]{2,1,0:T(8,128)(2,1)} %first_back.1), calls=%async_computation.1 | async-start | bytes 1572864 | tf_op jit(solution)/shard_map/all_to_all | solution.py:61
  192.3 3.0 %collective-permute-start.23 = (f32[6,768]{1,0:T(8,128)S(1)}, f32[6,768]{1,0:T(8,128)S(1)}, u32[]{:S(2)}, u32[]{:S(2)}) collective-permute-start(f32[6,768]{1,0:T(8,128)S(1)} %add.65), channel_id=1, source_target_pairs={{0,8},{4,12},{8,0},{12,4},{1,9},{5,13},{9,1},{13,5},{2,10},{6,14},... | collective-permute-start | bytes 55304 | tf_op jit(solution)/shard_map/ppermute | solution.py:26
  201.6 8.3 %collective-permute-start.24 = (bf16[2,104,768]{2,1,0:T(8,128)(2,1)S(1)}, bf16[2,104,768]{2,1,0:T(8,128)(2,1)S(1)}, u32[]{:S(2)}, u32[]{:S(2)}) collective-permute-start(bf16[2,104,768]{2,1,0:T(8,128)(2,1)S(1)} %get-tuple-element.166), channel_id=1, source_target_pairs={{0,8},{4,12},{8,0},{12,4},{1,9},{5,13},{9,1},{13,5},{2,10},{6,14},... | collective-permute-start | bytes 958472 | tf_op jit(solution)/shard_map/ppermute | solution.py:26
  203.9 8.0 %collective-permute-start.29 = (bf16[2,96,768]{2,1,0:T(8,128)(2,1)S(1)}, bf16[2,96,768]{2,1,0:T(8,128)(2,1)S(1)}, u32[]{:S(2)}, u32[]{:S(2)}) collective-permute-start(bf16[2,96,768]{2,1,0:T(8,128)(2,1)S(1)} %dynamic-slice_bitcast_fusion.2), channel_id=1, source_target_pairs={{0,16},{16,0},{1,17},{17,1},{2,18},{18,2},{3,19},{19,3},{4,20},{20... | collective-permute-start | bytes 884744 | tf_op jit(solution)/shard_map/ppermute | solution.py:26
  211.9 32.0 %collective-permute-start.30 = (bf16[192,768]{1,0:T(8,128)(2,1)S(1)}, bf16[192,768]{1,0:T(8,128)(2,1)S(1)}, u32[]{:S(2)}, u32[]{:S(2)}) collective-permute-start(bf16[192,768]{1,0:T(8,128)(2,1)S(1)} %bitcast.76), channel_id=1, source_target_pairs={{0,0},{4,1},{8,2},{12,3},{1,4},{5,5},{9,6},{13,7},{2,8},{6,9},{10,... | collective-permute-start | bytes 884744 | tf_op jit(solution)/shard_map/ppermute | solution.py:39
  216.5 10.2 %collective-permute-start.25 = (bf16[104,768]{1,0:T(8,128)(2,1)S(1)}, bf16[104,768]{1,0:T(8,128)(2,1)S(1)}, u32[]{:S(2)}, u32[]{:S(2)}) collective-permute-start(bf16[104,768]{1,0:T(8,128)(2,1)S(1)} %get-tuple-element.164), channel_id=1, source_target_pairs={{0,0},{1,4},{2,2},{3,6},{4,1},{5,5},{6,3},{7,7},{8,10},{9,14},{10,... | collective-permute-start | bytes 479240 | tf_op jit(solution)/shard_map/ppermute | solution.py:57
  218.5 8.3 %collective-permute-start.26 = (bf16[104,768]{1,0:T(8,128)(2,1)S(1)}, bf16[104,768]{1,0:T(8,128)(2,1)S(1)}, u32[]{:S(2)}, u32[]{:S(2)}) collective-permute-start(bf16[104,768]{1,0:T(8,128)(2,1)S(1)} %get-tuple-element.163), channel_id=1, source_target_pairs={{0,4},{1,0},{2,6},{3,2},{4,5},{5,1},{6,7},{7,3},{8,14},{9,10},{10,... | collective-permute-start | bytes 479240 | tf_op jit(solution)/shard_map/ppermute | solution.py:57
  218.5 14.1 %collective-permute-start.27 = (bf16[104,768]{1,0:T(8,128)(2,1)S(1)}, bf16[104,768]{1,0:T(8,128)(2,1)S(1)}, u32[]{:S(2)}, u32[]{:S(2)}) collective-permute-start(bf16[104,768]{1,0:T(8,128)(2,1)S(1)} %get-tuple-element.162), channel_id=1, source_target_pairs={{0,2},{1,6},{2,0},{3,4},{4,3},{5,7},{6,1},{7,5},{8,8},{9,12},{10,1... | collective-permute-start | bytes 479240 | tf_op jit(solution)/shard_map/ppermute | solution.py:57
  223.1 20.8 %collective-permute-start.28 = (bf16[104,768]{1,0:T(8,128)(2,1)S(1)}, bf16[104,768]{1,0:T(8,128)(2,1)S(1)}, u32[]{:S(2)}, u32[]{:S(2)}) collective-permute-start(bf16[104,768]{1,0:T(8,128)(2,1)S(1)} %get-tuple-element.161), channel_id=1, source_target_pairs={{0,6},{1,2},{2,4},{3,0},{4,7},{5,3},{6,5},{7,1},{8,12},{9,8},{10,1... | collective-permute-start | bytes 479240 | tf_op jit(solution)/shard_map/ppermute | solution.py:57
  (39 other events, 329.6 us)
Sparse Core Ops, SparseCore 0:
  52.5 60.9 all-gather.1
  141.4 46.0 reduce-scatter.1

commit v2 on v1

--- a/solution.py
+++ b/solution.py
@@ -104,7 +104,7 @@
 
 def cost(micros, nbytes):
     return pl.CostEstimate(
-        flops=int(micros * 0.2 * 10**9), transcendentals=0, bytes_accessed=1024
+        flops=int(micros * 0.27 * 10**9), transcendentals=0, bytes_accessed=1024
     )
 
 

time: 256 us -> 255 us (level)
  waiting for transfers between devices: 90.2 us -> 97.3 us
  local copies, waits for them, and re-layouts: 20.8 us -> 17.3 us
  starting transfers between devices: 72.5 us -> 69.6 us
    unnamed x76 -> x66, local copies, waits for them, and re-layouts: 15.2 us -> 10 us
    all_to_all x2, waiting for transfers between devices: 2.97 us -> 6.5 us  [rows_over_z(): return lax.all_to_all(arr, 'tp', 0, 0, tiled=True)]
    ppermute x1, starting transfers between devices: 4.51 us -> 1.92 us  [send_back(): return lax.ppermute(x, ('ctx', 'tp'), [(d, s) for s, d in pairs])]
  transfers between devices with their start and end apart: 35 -> 35, of which waited for: 22 -> 21; matrix products, arithmetic and copies ran while one was open for 2% -> 3% of each run, Pallas kernels for 18% -> 18%
where the time goes in v2:
time: 255 us; the launch traced here: 254 us
  waiting for transfers between devices  97.3 us (38%)
  starting transfers between devices  69.6 us (27%)
  Pallas kernels  49.6 us (19%)
  local copies, waits for them, and re-layouts  17.3 us (7%)
  between operations  14.8 us (6%)
  other arithmetic  5.36 us (2%)
    ppermute x21, waiting for transfers between devices, xor_swap(): return lax.ppermute(x, axis, [(i, i ^ k) for i in range(n)])  61.4 us
    ppermute x5, starting transfers between devices, send_turned(): return lax.ppermute(x, ('ctx', 'tp'), turn_pairs(lax.axis_size('tp'), k))  27.7 us
    ppermute x21, starting transfers between devices, xor_swap(): return lax.ppermute(x, axis, [(i, i ^ k) for i in range(n)])  24.2 us
    ppermute x4, waiting for transfers between devices, scatter_blocks(): lax.ppermute(pick(four, q ^ k), ('ctx', 'tp'), hop_pairs(n, k))  18.6 us
    pallas_call x1, Pallas kernels, attend_back(): pl.pallas_call(partial(attend_back_kernel, heads), out_shape=(jax.ShapeDt...  15.5 us
    unnamed x66, local copies, waits for them, and re-layouts  10 us
    pallas_call x1, Pallas kernels, attend(): pl.pallas_call(partial(attend_kernel, heads), out_shape=(jax.ShapeDtypeSt...  9.61 us
    ppermute x5, waiting for transfers between devices, send_turned(): return lax.ppermute(x, ('ctx', 'tp'), turn_pairs(lax.axis_size('tp'), k))  8.63 us
  transfers between devices with their start and end apart: 35, of which 21 were waited for; matrix products, arithmetic and copies ran while one was open for 3% of the time, Pallas kernels for 18%

profile of v2, /device:TPU:1, one launch (start us, length us, event | category | flops | bytes accessed | tf_op | source)
XLA Modules:
  0.0 254.0 jit_solution(787514396307579794)
XLA Ops:
  11.1 4.6 %collective-permute-start = (bf16[104,768]{1,0:T(8,128)(2,1)S(1)}, bf16[104,768]{1,0:T(8,128)(2,1)S(1)}, u32[]{:S(2)}, u32[]{:S(2)}) collective-permute-start(bf16[104,768]{1,0:T(8,128)(2,1)S(1)} %concatenate.35), channel_id=1, source_target_pairs={{0,0},{1,4},{2,8},{3,12},{4,1},{5,5},{6,9},{7,13},{8,2},{9,6},{10,... | collective-permute-start | bytes 479240 | tf_op jit(solution)/shard_map/ppermute | solution.py:34
  15.8 5.0 %collective-permute-start.2 = (bf16[104,768]{1,0:T(8,128)(2,1)S(1)}, bf16[104,768]{1,0:T(8,128)(2,1)S(1)}, u32[]{:S(2)}, u32[]{:S(2)}) collective-permute-start(bf16[104,768]{1,0:T(8,128)(2,1)S(1)} %concatenate.35), channel_id=1, source_target_pairs={{0,2},{1,6},{2,10},{3,14},{4,3},{5,7},{6,11},{7,15},{8,0},{9,4},{1... | collective-permute-start | bytes 479240 | tf_op jit(solution)/shard_map/ppermute | solution.py:34
  22.5 3.6 %all-to-all-start = ((bf16[4,136,768]{2,1,0:T(8,128)(2,1)}), bf16[4,136,768]{2,1,0:T(8,128)(2,1)S(1)}, u32[]{:S(2)}, u32[]{:S(2)}) async-start(bf16[4,136,768]{2,1,0:T(8,128)(2,1)} %fusion.3), calls=%async_computation | async-start | bytes 1671168 | tf_op jit(solution)/shard_map/all_to_all | solution.py:61
  26.3 2.1 collective-permute-done.3
  29.8 18.0 %collective-permute-start.10 = (bf16[192,768]{1,0:T(8,128)(2,1)S(1)}, bf16[192,768]{1,0:T(8,128)(2,1)S(1)}, u32[]{:S(2)}, u32[]{:S(2)}) collective-permute-start(bf16[192,768]{1,0:T(8,128)(2,1)S(1)} %pad_maximum_fusion.4), channel_id=1, source_target_pairs={{0,0},{1,4},{2,8},{3,12},{4,1},{5,5},{6,9},{7,13},{8,2},{9,6},{10,... | collective-permute-start | bytes 884744 | tf_op jit(solution)/shard_map/ppermute | solution.py:34
  47.8 6.5 %collective-permute-done.10 = bf16[192,768]{1,0:T(8,128)(2,1)S(1)} collective-permute-done((bf16[192,768]{1,0:T(8,128)(2,1)S(1)}, bf16[192,768]{1,0:T(8,128)(2,1)S(1)}, u32[]{:S(2)}, u32[]{:S(2)}) %collective-permute-start.10) | collective-permute-done | bytes 294944 | tf_op jit(solution)/shard_map/ppermute | solution.py:34
  57.6 7.1 %collective-permute-done.5 = bf16[1,4,72,768]{3,2,1,0:T(8,128)(2,1)S(1)} collective-permute-done((bf16[1,4,72,768]{3,2,1,0:T(8,128)(2,1)S(1)}, bf16[1,4,72,768]{3,2,1,0:T(8,128)(2,1)S(1)}, u32[]{:S(2)}, u32[]{:S(2)}) %collective-permute-start.5) | collective-permute-done | bytes 442400 | tf_op jit(solution)/shard_map/ppermute | solution.py:26
  64.8 8.2 %collective-permute-start.6 = (bf16[2,4,72,768]{3,2,1,0:T(8,128)(2,1)S(1)}, bf16[2,4,72,768]{3,2,1,0:T(8,128)(2,1)S(1)}, u32[]{:S(2)}, u32[]{:S(2)}) collective-permute-start(bf16[2,4,72,768]{3,2,1,0:T(8,128)(2,1)S(1)} %pad_maximum_fusion.1.xo_ref.x_ref), channel_id=1, source_target_pairs={{0,4},{4,0},{8,12},{12,8},{1,5},{5,1},{9,13},{13,9},{2,6},{6,2},{1... | collective-permute-start | bytes 2654216 | tf_op jit(solution)/shard_map/ppermute | solution.py:26
  76.7 2.6 %qkv.1 = (bf16[4,4,64,768]{3,2,1,0:T(8,128)(2,1)S(1)}, f32[8,1024]{1,0:T(8,128)S(1)}, s32[4]{0:T(128)S(1)}, s32[4]{0:T(128)S(1)}) custom-call(bf16[2,4,72,768]{3,2,1,0:T(8,128)(2,1)S(1)} %pad_maximum_fusion.1.xo_ref.x_ref, bf16[2,4,72,768]{3,2,1,0:T(8,128)(2,1)S(1)} %collective-permute-done.6.xp_ref, f32[6,768]{1,0:T(8,128)S(1)} %stack.43.vec_ref, ...), custom_call_target="tpu_custom_call" | custom-call | flops 1080000000 | bytes 1024 | tf_op jit(solution)/shard_map/qkv/pallas_call | solution.py:174
  79.3 9.6 %attend.1 = (bf16[4,4,64,192]{3,2,1,0:T(8,128)(2,1)S(1)}, f32[8,1024]{1,0:T(8,128)S(1)}, f32[2,4,64,768]{3,2,1,0:T(8,128)S(1)}, bf16[2,4,64,768]{3,2,1,0:T(8,128)(2,1)S(1)}) custom-call(s32[4]{0:T(128)S(1)} %get-tuple-element.70.lo_ref, s32[4]{0:T(128)S(1)} %get-tuple-element.71.hi_ref, bf16[4,4,64,768]{3,2,1,0:T(8,128)(2,1)S(1)} %get-tuple-element.72.qkv_ref, ...), custom_call_target="tpu_custom_call" | custom-call | flops 2969999872 | bytes 1024 | tf_op jit(solution)/shard_map/attend/pallas_call | solution.py:337
  89.3 2.0 collective-permute-done.8.got_ref
  93.6 16.9 %collective-permute-done.9.got_ref = bf16[2,4,64,768]{3,2,1,0:T(8,128)(2,1)S(1)} collective-permute-done((bf16[2,4,64,768]{3,2,1,0:T(8,128)(2,1)S(1)}, bf16[2,4,64,768]{3,2,1,0:T(8,128)(2,1)S(1)}, u32[]{:S(2)}, u32[]{:S(2)}) %collective-permute-start.9) | collective-permute-done | bytes 786464 | tf_op jit(solution)/shard_map/ppermute | solution.py:26
  111.4 2.2 all-gather.2.cloned.1.call-done
  115.6 1.9 collective-permute-start.11
  119.4 4.2 %mlp_block.1 = (bf16[1024,768]{1,0:T(8,128)(2,1)S(1)}, bf16[1024,768]{1,0:T(8,128)(2,1)S(1)}, f32[2,4,64,768]{3,2,1,0:T(8,128)S(1)}, bf16[2,4,64,768]{3,2,1,0:T(8,128)(2,1)S(1)}) custom-call(bf16[2,4,64,768]{3,2,1,0:T(8,128)(2,1)S(1)} %get-tuple-element.83.xo_ref, bf16[2,4,64,768]{3,2,1,0:T(8,128)(2,1)S(1)} %collective-permute-done.11.xp_ref, ...), custom_call_target="tpu_custom_call" | custom-call | flops 1890000000 | bytes 1024 | tf_op jit(solution)/shard_map/mlp_block/pallas_call | solution.py:667
  124.1 1.9 collective-permute-done.13.got_ref
  127.5 5.9 %mlp_grads.1 = (bf16[4,2,2,96,768]{4,3,2,1,0:T(8,128)(2,1)S(1)}, f32[2,4,64,768]{3,2,1,0:T(8,128)S(1)}, bf16[2,4,64,768]{3,2,1,0:T(8,128)(2,1)}, f32[1,768]{1,0:T(1,128)S(1)}) custom-call(bf16[2,4,64,768]{3,2,1,0:T(8,128)(2,1)S(1)} %get-tuple-element.83.xo_ref, bf16[2,4,64,768]{3,2,1,0:T(8,128)(2,1)S(1)} %collective-permute-done.11.xp_ref, ...), custom_call_target="tpu_custom_call" | custom-call | flops 1620000000 | bytes 1024 | tf_op jit(solution)/shard_map/mlp_grads/pallas_call | solution.py:720
  133.4 11.7 %collective-permute-done.14.got_ref = bf16[2,4,64,768]{3,2,1,0:T(8,128)(2,1)S(1)} collective-permute-done((bf16[2,4,64,768]{3,2,1,0:T(8,128)(2,1)S(1)}, bf16[2,4,64,768]{3,2,1,0:T(8,128)(2,1)S(1)}, u32[]{:S(2)}, u32[]{:S(2)}) %collective-permute-start.14) | collective-permute-done | bytes 786464 | tf_op jit(solution)/shard_map/ppermute | solution.py:26
  146.3 2.3 middle_back.1
  154.9 15.5 %attend_back.1 = (bf16[4,4,64,768]{3,2,1,0:T(8,128)(2,1)S(1)}, f32[2,4,64,768]{3,2,1,0:T(8,128)S(1)}, bf16[2,4,64,768]{3,2,1,0:T(8,128)(2,1)S(1)}) custom-call(s32[4]{0:T(128)S(1)} %get-tuple-element.70.lo_ref, s32[4]{0:T(128)S(1)} %get-tuple-element.71.hi_ref, bf16[4,4,64,768]{3,2,1,0:T(8,128)(2,1)S(1)} %copy-done.17, ...), custom_call_target="tpu_custom_call" | custom-call | flops 18900000768 | bytes 1024 | tf_op jit(solution)/shard_map/attend_back/pallas_call | solution.py:459
  173.4 5.0 %attend_grads.1 = (bf16[392,768]{1,0:T(8,128)(2,1)S(1)}, bf16[392,768]{1,0:T(8,128)(2,1)S(1)}, f32[2,768]{1,0:T(2,128)S(1)}) custom-call(s32[1]{0:T(128)} %bitcast.14.flip_ref, f32[1,768]{1,0:T(1,128)S(1)} %get-tuple-element.90.sum_ref, f32[2,768]{1,0:T(2,128)S(1)} %get-tuple-element.171.norm_ref, bf16[1024,768]{1,0:T(8,128)(2,1)S(1)} %bitcast.64, ...), custom_call_target="tpu_custom_call" | custom-call | flops 1620000000 | bytes 1024 | tf_op jit(solution)/shard_map/attend_grads/pallas_call | solution.py:796
  178.6 2.9 %collective-permute-done.20 = f32[6,768]{1,0:T(8,128)S(1)} collective-permute-done((f32[6,768]{1,0:T(8,128)S(1)}, f32[6,768]{1,0:T(8,128)S(1)}, u32[]{:S(2)}, u32[]{:S(2)}) %collective-permute-start.20) | collective-permute-done | bytes 18464 | tf_op jit(solution)/shard_map/ppermute | solution.py:26
  185.7 3.5 %all-to-all-start.1 = ((bf16[4,128,768]{2,1,0:T(8,128)(2,1)}), bf16[4,128,768]{2,1,0:T(8,128)(2,1)S(1)}, u32[]{:S(2)}, u32[]{:S(2)}) async-start(bf16[4,128,768]{2,1,0:T(8,128)(2,1)} %first_back.1), calls=%async_computation.1 | async-start | bytes 1572864 | tf_op jit(solution)/shard_map/all_to_all | solution.py:61
  192.3 5.9 %collective-permute-done.22.got_ref = bf16[392,768]{1,0:T(8,128)(2,1)S(1)} collective-permute-done((bf16[392,768]{1,0:T(8,128)(2,1)S(1)}, bf16[392,768]{1,0:T(8,128)(2,1)S(1)}, u32[]{:S(2)}, u32[]{:S(2)}) %collective-permute-start.22) | collective-permute-done | bytes 602144 | tf_op jit(solution)/shard_map/ppermute | solution.py:26
  201.1 5.6 %collective-permute-done.24 = bf16[2,104,768]{2,1,0:T(8,128)(2,1)S(1)} collective-permute-done((bf16[2,104,768]{2,1,0:T(8,128)(2,1)S(1)}, bf16[2,104,768]{2,1,0:T(8,128)(2,1)S(1)}, u32[]{:S(2)}, u32[]{:S(2)}) %collective-permute-start.24) | collective-permute-done | bytes 319520 | tf_op jit(solution)/shard_map/ppermute | solution.py:26
  206.8 5.3 %all-to-all-done.1 = bf16[4,128,768]{2,1,0:T(8,128)(2,1)S(1)} async-done(((bf16[4,128,768]{2,1,0:T(8,128)(2,1)}), bf16[4,128,768]{2,1,0:T(8,128)(2,1)S(1)}, u32[]{:S(2)}, u32[]{:S(2)}) %all-to-all-start.1) | async-done | bytes 786464 | tf_op jit(solution)/shard_map/all_to_all | solution.py:61
  212.1 1.9 collective-permute-start.30
  214.1 3.6 %collective-permute-start.25 = (bf16[104,768]{1,0:T(8,128)(2,1)S(1)}, bf16[104,768]{1,0:T(8,128)(2,1)S(1)}, u32[]{:S(2)}, u32[]{:S(2)}) collective-permute-start(bf16[104,768]{1,0:T(8,128)(2,1)S(1)} %get-tuple-element.164), channel_id=1, source_target_pairs={{0,0},{1,4},{2,2},{3,6},{4,1},{5,5},{6,3},{7,7},{8,10},{9,14},{10,... | collective-permute-start | bytes 479240 | tf_op jit(solution)/shard_map/ppermute | solution.py:57
  217.9 4.7 %collective-permute-start.27 = (bf16[104,768]{1,0:T(8,128)(2,1)S(1)}, bf16[104,768]{1,0:T(8,128)(2,1)S(1)}, u32[]{:S(2)}, u32[]{:S(2)}) collective-permute-start(bf16[104,768]{1,0:T(8,128)(2,1)S(1)} %get-tuple-element.162), channel_id=1, source_target_pairs={{0,2},{1,6},{2,0},{3,4},{4,3},{5,7},{6,1},{7,5},{8,8},{9,12},{10,1... | collective-permute-start | bytes 479240 | tf_op jit(solution)/shard_map/ppermute | solution.py:57
  223.8 2.2 collective-permute-done.25
  226.0 5.6 %collective-permute-done.27 = bf16[104,768]{1,0:T(8,128)(2,1)S(1)} collective-permute-done((bf16[104,768]{1,0:T(8,128)(2,1)S(1)}, bf16[104,768]{1,0:T(8,128)(2,1)S(1)}, u32[]{:S(2)}, u32[]{:S(2)}) %collective-permute-start.27) | collective-permute-done | bytes 159776 | tf_op jit(solution)/shard_map/ppermute | solution.py:57
  231.6 10.8 %collective-permute-done.28 = bf16[104,768]{1,0:T(8,128)(2,1)S(1)} collective-permute-done((bf16[104,768]{1,0:T(8,128)(2,1)S(1)}, bf16[104,768]{1,0:T(8,128)(2,1)S(1)}, u32[]{:S(2)}, u32[]{:S(2)}) %collective-permute-start.28) | collective-permute-done | bytes 159776 | tf_op jit(solution)/shard_map/ppermute | solution.py:57
  (175 shorter events, 50.3 us)
Async XLA Ops:
  11.1 15.1 %collective-permute-start = (bf16[104,768]{1,0:T(8,128)(2,1)S(1)}, bf16[104,768]{1,0:T(8,128)(2,1)S(1)}, u32[]{:S(2)}, u32[]{:S(2)}) collective-permute-start(bf16[104,768]{1,0:T(8,128)(2,1)S(1)} %concatenate.35), channel_id=1, source_target_pairs={{0,0},{1,4},{2,8},{3,12},{4,1},{5,5},{6,9},{7,13},{8,2},{9,6},{10,... | collective-permute-start | bytes 479240 | tf_op jit(solution)/shard_map/ppermute | solution.py:34
  15.7 10.5 %collective-permute-start.1 = (bf16[104,768]{1,0:T(8,128)(2,1)S(1)}, bf16[104,768]{1,0:T(8,128)(2,1)S(1)}, u32[]{:S(2)}, u32[]{:S(2)}) collective-permute-start(bf16[104,768]{1,0:T(8,128)(2,1)S(1)} %concatenate.35), channel_id=1, source_target_pairs={{0,1},{1,5},{2,9},{3,13},{4,0},{5,4},{6,8},{7,12},{8,3},{9,7},{10,... | collective-permute-start | bytes 479240 | tf_op jit(solution)/shard_map/ppermute | solution.py:34
  15.8 10.5 %collective-permute-start.2 = (bf16[104,768]{1,0:T(8,128)(2,1)S(1)}, bf16[104,768]{1,0:T(8,128)(2,1)S(1)}, u32[]{:S(2)}, u32[]{:S(2)}) collective-permute-start(bf16[104,768]{1,0:T(8,128)(2,1)S(1)} %concatenate.35), channel_id=1, source_target_pairs={{0,2},{1,6},{2,10},{3,14},{4,3},{5,7},{6,11},{7,15},{8,0},{9,4},{1... | collective-permute-start | bytes 479240 | tf_op jit(solution)/shard_map/ppermute | solution.py:34
  20.8 7.6 %collective-permute-start.3 = (bf16[104,768]{1,0:T(8,128)(2,1)S(1)}, bf16[104,768]{1,0:T(8,128)(2,1)S(1)}, u32[]{:S(2)}, u32[]{:S(2)}) collective-permute-start(bf16[104,768]{1,0:T(8,128)(2,1)S(1)} %concatenate.35), channel_id=1, source_target_pairs={{0,3},{1,7},{2,11},{3,15},{4,2},{5,6},{6,10},{7,14},{8,1},{9,5},{1... | collective-permute-start | bytes 479240 | tf_op jit(solution)/shard_map/ppermute | solution.py:34
  22.5 34.2 %all-to-all-start = ((bf16[4,136,768]{2,1,0:T(8,128)(2,1)}), bf16[4,136,768]{2,1,0:T(8,128)(2,1)S(1)}, u32[]{:S(2)}, u32[]{:S(2)}) async-start(bf16[4,136,768]{2,1,0:T(8,128)(2,1)} %fusion.3), calls=%async_computation | async-start | bytes 1671168 | tf_op jit(solution)/shard_map/all_to_all | solution.py:61
  26.1 87.4 %all-gather.2.cloned.1.call-start = ((), (), s32[]{:S(2)}) async-start(), calls=%async_computation.3 | async-start | bytes 2654208 | tf_op jit(solution)/shard_map/all_gather | solution.py:859
  28.5 26.7 %collective-permute-start.4 = (bf16[384,768]{1,0:T(8,128)(2,1)S(1)}, bf16[384,768]{1,0:T(8,128)(2,1)S(1)}, u32[]{:S(2)}, u32[]{:S(2)}) collective-permute-start(bf16[384,768]{1,0:T(8,128)(2,1)S(1)} %bitcast.67), channel_id=1, source_target_pairs={{0,16},{16,0},{1,17},{17,1},{2,18},{18,2},{3,19},{19,3},{4,20},{20... | collective-permute-start | bytes 1769480 | tf_op jit(solution)/shard_map/ppermute | solution.py:26
  29.8 24.6 %collective-permute-start.10 = (bf16[192,768]{1,0:T(8,128)(2,1)S(1)}, bf16[192,768]{1,0:T(8,128)(2,1)S(1)}, u32[]{:S(2)}, u32[]{:S(2)}) collective-permute-start(bf16[192,768]{1,0:T(8,128)(2,1)S(1)} %pad_maximum_fusion.4), channel_id=1, source_target_pairs={{0,0},{1,4},{2,8},{3,12},{4,1},{5,5},{6,9},{7,13},{8,2},{9,6},{10,... | collective-permute-start | bytes 884744 | tf_op jit(solution)/shard_map/ppermute | solution.py:34
  55.1 144.7 %reduce-scatter.2.cloned.1.call-start = ((), (), s32[]{:S(2)}) async-start(), calls=%async_computation.4 | async-start | bytes 2949120 | tf_op jit(solution)/shard_map/reduce_scatter | solution.py:891
  56.7 8.0 %collective-permute-start.5 = (bf16[1,4,72,768]{3,2,1,0:T(8,128)(2,1)S(1)}, bf16[1,4,72,768]{3,2,1,0:T(8,128)(2,1)S(1)}, u32[]{:S(2)}, u32[]{:S(2)}) collective-permute-start(bf16[1,4,72,768]{3,2,1,0:T(8,128)(2,1)S(1)} %bitcast.68), channel_id=1, source_target_pairs={{0,8},{4,12},{8,0},{12,4},{1,9},{5,13},{9,1},{13,5},{2,10},{6,14},... | collective-permute-start | bytes 1327112 | tf_op jit(solution)/shard_map/ppermute | solution.py:26
  64.8 11.9 %collective-permute-start.6 = (bf16[2,4,72,768]{3,2,1,0:T(8,128)(2,1)S(1)}, bf16[2,4,72,768]{3,2,1,0:T(8,128)(2,1)S(1)}, u32[]{:S(2)}, u32[]{:S(2)}) collective-permute-start(bf16[2,4,72,768]{3,2,1,0:T(8,128)(2,1)S(1)} %pad_maximum_fusion.1.xo_ref.x_ref), channel_id=1, source_target_pairs={{0,4},{4,0},{8,12},{12,8},{1,5},{5,1},{9,13},{13,9},{2,6},{6,2},{1... | collective-permute-start | bytes 2654216 | tf_op jit(solution)/shard_map/ppermute | solution.py:26
  74.8 14.2 %collective-permute-start.7 = (bf16[1,4,64,768]{3,2,1,0:T(8,128)(2,1)}, bf16[1,4,64,768]{3,2,1,0:T(8,128)(2,1)}, u32[]{:S(2)}, u32[]{:S(2)}) collective-permute-start(bf16[1,4,64,768]{3,2,1,0:T(8,128)(2,1)} %bitcast.11), channel_id=1, source_target_pairs={{0,8},{4,12},{8,0},{12,4},{1,9},{5,13},{9,1},{13,5},{2,10},{6,14},... | collective-permute-start | bytes 1179656 | tf_op jit(solution)/shard_map/ppermute | solution.py:26
  91.5 19.0 %collective-permute-start.9 = (bf16[2,4,64,768]{3,2,1,0:T(8,128)(2,1)S(1)}, bf16[2,4,64,768]{3,2,1,0:T(8,128)(2,1)S(1)}, u32[]{:S(2)}, u32[]{:S(2)}) collective-permute-start(bf16[2,4,64,768]{3,2,1,0:T(8,128)(2,1)S(1)} %add_rows.4.s_ref), channel_id=1, source_target_pairs={{0,8},{4,12},{8,0},{12,4},{1,9},{5,13},{9,1},{13,5},{2,10},{6,14},... | collective-permute-start | bytes 2359304 | tf_op jit(solution)/shard_map/ppermute | solution.py:26
  92.9 24.7 %collective-permute-start.12 = (bf16[2,4,64,768]{3,2,1,0:T(8,128)(2,1)S(1)}, bf16[2,4,64,768]{3,2,1,0:T(8,128)(2,1)S(1)}, u32[]{:S(2)}, u32[]{:S(2)}) collective-permute-start(bf16[2,4,64,768]{3,2,1,0:T(8,128)(2,1)S(1)} %pad_maximum_fusion.2.go_ref.g_ref), channel_id=1, source_target_pairs={{0,4},{4,0},{8,12},{12,8},{1,5},{5,1},{9,13},{13,9},{2,6},{6,2},{1... | collective-permute-start | bytes 2359304 | tf_op jit(solution)/shard_map/ppermute | solution.py:26
  115.6 3.8 %collective-permute-start.11 = (bf16[2,4,64,768]{3,2,1,0:T(8,128)(2,1)S(1)}, bf16[2,4,64,768]{3,2,1,0:T(8,128)(2,1)S(1)}, u32[]{:S(2)}, u32[]{:S(2)}) collective-permute-start(bf16[2,4,64,768]{3,2,1,0:T(8,128)(2,1)S(1)} %get-tuple-element.83.xo_ref), channel_id=1, source_target_pairs={{0,4},{4,0},{8,12},{12,8},{1,5},{5,1},{9,13},{13,9},{2,6},{6,2},{1... | collective-permute-start | bytes 2359304 | tf_op jit(solution)/shard_map/ppermute | solution.py:26
  126.3 18.8 %collective-permute-start.14 = (bf16[2,4,64,768]{3,2,1,0:T(8,128)(2,1)S(1)}, bf16[2,4,64,768]{3,2,1,0:T(8,128)(2,1)S(1)}, u32[]{:S(2)}, u32[]{:S(2)}) collective-permute-start(bf16[2,4,64,768]{3,2,1,0:T(8,128)(2,1)S(1)} %add_rows.5.s_ref), channel_id=1, source_target_pairs={{0,8},{4,12},{8,0},{12,4},{1,9},{5,13},{9,1},{13,5},{2,10},{6,14},... | collective-permute-start | bytes 2359304 | tf_op jit(solution)/shard_map/ppermute | solution.py:26
  145.1 4.7 %collective-permute-start.16 = (bf16[2,4,64,768]{3,2,1,0:T(8,128)(2,1)}, bf16[2,4,64,768]{3,2,1,0:T(8,128)(2,1)}, u32[]{:S(2)}, u32[]{:S(2)}) collective-permute-start(bf16[2,4,64,768]{3,2,1,0:T(8,128)(2,1)} %get-tuple-element.98), channel_id=1, source_target_pairs={{0,4},{4,0},{8,12},{12,8},{1,5},{5,1},{9,13},{13,9},{2,6},{6,2},{1... | collective-permute-start | bytes 2359304 | tf_op jit(solution)/shard_map/ppermute | solution.py:26
  149.7 2.5 collective-permute-start.15
  152.2 18.2 %collective-permute-start.17 = (bf16[1,4,64,768]{3,2,1,0:T(8,128)(2,1)S(1)}, bf16[1,4,64,768]{3,2,1,0:T(8,128)(2,1)S(1)}, u32[]{:S(2)}, u32[]{:S(2)}) collective-permute-start(bf16[1,4,64,768]{3,2,1,0:T(8,128)(2,1)S(1)} %get-tuple-element.100), channel_id=1, source_target_pairs={{0,8},{4,12},{8,0},{12,4},{1,9},{5,13},{9,1},{13,5},{2,10},{6,14},... | collective-permute-start | bytes 1179656 | tf_op jit(solution)/shard_map/ppermute | solution.py:26
  170.4 2.5 %collective-permute-start.18 = (bf16[2,4,64,768]{3,2,1,0:T(8,128)(2,1)S(1)}, bf16[2,4,64,768]{3,2,1,0:T(8,128)(2,1)S(1)}, u32[]{:S(2)}, u32[]{:S(2)}) collective-permute-start(bf16[2,4,64,768]{3,2,1,0:T(8,128)(2,1)S(1)} %get-tuple-element.101.sent_ref), channel_id=1, source_target_pairs={{0,4},{4,0},{8,12},{12,8},{1,5},{5,1},{9,13},{13,9},{2,6},{6,2},{1... | collective-permute-start | bytes 2359304 | tf_op jit(solution)/shard_map/ppermute | solution.py:26
  173.2 10.7 %collective-permute-start.19 = (bf16[1,4,64,768]{3,2,1,0:T(8,128)(2,1)S(1)}, bf16[1,4,64,768]{3,2,1,0:T(8,128)(2,1)S(1)}, u32[]{:S(2)}, u32[]{:S(2)}) collective-permute-start(bf16[1,4,64,768]{3,2,1,0:T(8,128)(2,1)S(1)} %get-tuple-element.103), channel_id=1, source_target_pairs={{0,8},{4,12},{8,0},{12,4},{1,9},{5,13},{9,1},{13,5},{2,10},{6,14},... | collective-permute-start | bytes 1179656 | tf_op jit(solution)/shard_map/ppermute | solution.py:26
  178.4 3.1 %collective-permute-start.20 = (f32[6,768]{1,0:T(8,128)S(1)}, f32[6,768]{1,0:T(8,128)S(1)}, u32[]{:S(2)}, u32[]{:S(2)}) collective-permute-start(f32[6,768]{1,0:T(8,128)S(1)} %pad_maximum_fusion.6), channel_id=1, source_target_pairs={{0,16},{16,0},{1,17},{17,1},{2,18},{18,2},{3,19},{19,3},{4,20},{20... | collective-permute-start | bytes 55304 | tf_op jit(solution)/shard_map/ppermute | solution.py:26
  183.1 15.2 %collective-permute-start.22 = (bf16[392,768]{1,0:T(8,128)(2,1)S(1)}, bf16[392,768]{1,0:T(8,128)(2,1)S(1)}, u32[]{:S(2)}, u32[]{:S(2)}) collective-permute-start(bf16[392,768]{1,0:T(8,128)(2,1)S(1)} %get-tuple-element.112), channel_id=1, source_target_pairs={{0,16},{16,0},{1,17},{17,1},{2,18},{18,2},{3,19},{19,3},{4,20},{20... | collective-permute-start | bytes 1806344 | tf_op jit(solution)/shard_map/ppermute | solution.py:26
  185.7 26.4 %all-to-all-start.1 = ((bf16[4,128,768]{2,1,0:T(8,128)(2,1)}), bf16[4,128,768]{2,1,0:T(8,128)(2,1)S(1)}, u32[]{:S(2)}, u32[]{:S(2)}) async-start(bf16[4,128,768]{2,1,0:T(8,128)(2,1)} %first_back.1), calls=%async_computation.1 | async-start | bytes 1572864 | tf_op jit(solution)/shard_map/all_to_all | solution.py:61
  189.2 3.1 %collective-permute-start.23 = (f32[6,768]{1,0:T(8,128)S(1)}, f32[6,768]{1,0:T(8,128)S(1)}, u32[]{:S(2)}, u32[]{:S(2)}) collective-permute-start(f32[6,768]{1,0:T(8,128)S(1)} %add.65), channel_id=1, source_target_pairs={{0,8},{4,12},{8,0},{12,4},{1,9},{5,13},{9,1},{13,5},{2,10},{6,14},... | collective-permute-start | bytes 55304 | tf_op jit(solution)/shard_map/ppermute | solution.py:26
  198.4 8.3 %collective-permute-start.24 = (bf16[2,104,768]{2,1,0:T(8,128)(2,1)S(1)}, bf16[2,104,768]{2,1,0:T(8,128)(2,1)S(1)}, u32[]{:S(2)}, u32[]{:S(2)}) collective-permute-start(bf16[2,104,768]{2,1,0:T(8,128)(2,1)S(1)} %get-tuple-element.166), channel_id=1, source_target_pairs={{0,8},{4,12},{8,0},{12,4},{1,9},{5,13},{9,1},{13,5},{2,10},{6,14},... | collective-permute-start | bytes 958472 | tf_op jit(solution)/shard_map/ppermute | solution.py:26
  200.9 11.2 %collective-permute-start.29 = (bf16[2,96,768]{2,1,0:T(8,128)(2,1)S(1)}, bf16[2,96,768]{2,1,0:T(8,128)(2,1)S(1)}, u32[]{:S(2)}, u32[]{:S(2)}) collective-permute-start(bf16[2,96,768]{2,1,0:T(8,128)(2,1)S(1)} %dynamic-slice_bitcast_fusion.2), channel_id=1, source_target_pairs={{0,16},{16,0},{1,17},{17,1},{2,18},{18,2},{3,19},{19,3},{4,20},{20... | collective-permute-start | bytes 884744 | tf_op jit(solution)/shard_map/ppermute | solution.py:26
  212.1 30.2 %collective-permute-start.30 = (bf16[192,768]{1,0:T(8,128)(2,1)S(1)}, bf16[192,768]{1,0:T(8,128)(2,1)S(1)}, u32[]{:S(2)}, u32[]{:S(2)}) collective-permute-start(bf16[192,768]{1,0:T(8,128)(2,1)S(1)} %bitcast.73), channel_id=1, source_target_pairs={{0,0},{4,1},{8,2},{12,3},{1,4},{5,5},{9,6},{13,7},{2,8},{6,9},{10,... | collective-permute-start | bytes 884744 | tf_op jit(solution)/shard_map/ppermute | solution.py:39
  214.1 11.9 %collective-permute-start.25 = (bf16[104,768]{1,0:T(8,128)(2,1)S(1)}, bf16[104,768]{1,0:T(8,128)(2,1)S(1)}, u32[]{:S(2)}, u32[]{:S(2)}) collective-permute-start(bf16[104,768]{1,0:T(8,128)(2,1)S(1)} %get-tuple-element.164), channel_id=1, source_target_pairs={{0,0},{1,4},{2,2},{3,6},{4,1},{5,5},{6,3},{7,7},{8,10},{9,14},{10,... | collective-permute-start | bytes 479240 | tf_op jit(solution)/shard_map/ppermute | solution.py:57
  217.8 8.2 %collective-permute-start.26 = (bf16[104,768]{1,0:T(8,128)(2,1)S(1)}, bf16[104,768]{1,0:T(8,128)(2,1)S(1)}, u32[]{:S(2)}, u32[]{:S(2)}) collective-permute-start(bf16[104,768]{1,0:T(8,128)(2,1)S(1)} %get-tuple-element.163), channel_id=1, source_target_pairs={{0,4},{1,0},{2,6},{3,2},{4,5},{5,1},{6,7},{7,3},{8,14},{9,10},{10,... | collective-permute-start | bytes 479240 | tf_op jit(solution)/shard_map/ppermute | solution.py:57
  217.9 13.8 %collective-permute-start.27 = (bf16[104,768]{1,0:T(8,128)(2,1)S(1)}, bf16[104,768]{1,0:T(8,128)(2,1)S(1)}, u32[]{:S(2)}, u32[]{:S(2)}) collective-permute-start(bf16[104,768]{1,0:T(8,128)(2,1)S(1)} %get-tuple-element.162), channel_id=1, source_target_pairs={{0,2},{1,6},{2,0},{3,4},{4,3},{5,7},{6,1},{7,5},{8,8},{9,12},{10,1... | collective-permute-start | bytes 479240 | tf_op jit(solution)/shard_map/ppermute | solution.py:57
  222.6 19.8 %collective-permute-start.28 = (bf16[104,768]{1,0:T(8,128)(2,1)S(1)}, bf16[104,768]{1,0:T(8,128)(2,1)S(1)}, u32[]{:S(2)}, u32[]{:S(2)}) collective-permute-start(bf16[104,768]{1,0:T(8,128)(2,1)S(1)} %get-tuple-element.161), channel_id=1, source_target_pairs={{0,6},{1,2},{2,4},{3,0},{4,7},{5,3},{6,5},{7,1},{8,12},{9,8},{10,1... | collective-permute-start | bytes 479240 | tf_op jit(solution)/shard_map/ppermute | solution.py:57
  (34 other events, 325.3 us)
Sparse Core Ops, SparseCore 0:
  55.2 58.2 all-gather.1
  149.9 46.7 reduce-scatter.1

commit v3 on v2

--- a/solution.py
+++ b/solution.py
@@ -497,7 +497,7 @@
 def middle_rows(s, got, x, vec):
     return pl.pallas_call(
         middle_kernel,
-        out_shape=(jax.ShapeDtypeStruct(s.shape, F32), jax.ShapeDtypeStruct(s.shape, BF)),
+        out_shape=(jax.ShapeDtypeStruct(s.shape, BF), jax.ShapeDtypeStruct(s.shape, BF)),
         in_specs=[VMEM] * 4,
         out_specs=(VMEM,) * 2,
         compiler_params=params(8),
@@ -511,15 +511,15 @@
 
     def step(i, carry):
         dxb = group(s_ref, i).astype(F32) + group(got_ref, n - 1 - i).astype(F32)
-        normal, rstd = normed(group(mid_ref, i))
+        normal, rstd = normed(group(mid_ref, i).astype(F32))
         grad = group(g_ref, i).astype(F32)
         dmid = grad + normed_back(dxb, normal, rstd, vec_ref[...])
         low = dmid.astype(BF)
-        put_rows(dmid_ref, i, dmid)
         put_rows(db_ref, i, low)
 
         @pl.when(i == 0)
         def _():
+            put_rows(dmid_ref, 0, dmid)
             sum_ref[0:1, :] = jnp.sum(low.astype(F32), 0, keepdims=True)
             sum_ref[1:2, :] = jnp.sum(dxb * normal, 0, keepdims=True)
             sum_ref[2:3, :] = jnp.sum(dxb, 0, keepdims=True)
@@ -534,7 +534,7 @@
     return pl.pallas_call(
         middle_back_kernel,
         out_shape=(
-            jax.ShapeDtypeStruct(s.shape, F32),
+            jax.ShapeDtypeStruct((1,) + s.shape[1:], F32),
             jax.ShapeDtypeStruct(s.shape, BF),
             jax.ShapeDtypeStruct((4, s.shape[-1]), F32),
         ),
@@ -572,7 +572,7 @@
 ):
     thin = s_ref.shape[2]
     pieces = out_ref.shape[0]
-    result = group(mid_ref, 0) + group(mlp_ref, 0).astype(F32) + group(mlpgot_ref, 0).astype(F32)
+    result = group(mid_ref, 0).astype(F32) + group(mlp_ref, 0).astype(F32) + group(mlpgot_ref, 0).astype(F32)
     result = result + vec_ref[1:2, :]
     out_ref[:, :thin, :] = result.astype(BF).reshape(pieces, thin, -1)
     dxa = group(s_ref, 0).astype(F32) + group(got_ref, 0).astype(F32)

time: 255 us -> 255 us (level)
  no operation moved by 1% of the time
where the time goes in v3:
time: 255 us; the launch traced here: 254 us
  waiting for transfers between devices  96.7 us (38%)
  starting transfers between devices  69.5 us (27%)
  Pallas kernels  50.7 us (20%)
  local copies, waits for them, and re-layouts  17.1 us (7%)
  between operations  14.7 us (6%)
  other arithmetic  5.36 us (2%)
    ppermute x21, waiting for transfers between devices, xor_swap(): return lax.ppermute(x, axis, [(i, i ^ k) for i in range(n)])  61.6 us
    ppermute x5, starting transfers between devices, send_turned(): return lax.ppermute(x, ('ctx', 'tp'), turn_pairs(lax.axis_size('tp'), k))  27.7 us
    ppermute x21, starting transfers between devices, xor_swap(): return lax.ppermute(x, axis, [(i, i ^ k) for i in range(n)])  24.1 us
    ppermute x4, waiting for transfers between devices, scatter_blocks(): lax.ppermute(pick(four, q ^ k), ('ctx', 'tp'), hop_pairs(n, k))  18.5 us
    pallas_call x1, Pallas kernels, attend_back(): pl.pallas_call(partial(attend_back_kernel, heads), out_shape=(jax.ShapeDt...  15.5 us
    unnamed x66, local copies, waits for them, and re-layouts  9.79 us
    pallas_call x1, Pallas kernels, attend(): pl.pallas_call(partial(attend_kernel, heads), out_shape=(jax.ShapeDtypeSt...  9.61 us
    ppermute x5, waiting for transfers between devices, send_turned(): return lax.ppermute(x, ('ctx', 'tp'), turn_pairs(lax.axis_size('tp'), k))  8.63 us
  transfers between devices with their start and end apart: 35, of which 21 were waited for; matrix products, arithmetic and copies ran while one was open for 3% of the time, Pallas kernels for 18%

profile of v3, /device:TPU:1, one launch (start us, length us, event | category | flops | bytes accessed | tf_op | source)
XLA Modules:
  0.0 254.1 jit_solution(9595054976708804208)
XLA Ops:
  11.1 4.6 %collective-permute-start = (bf16[104,768]{1,0:T(8,128)(2,1)S(1)}, bf16[104,768]{1,0:T(8,128)(2,1)S(1)}, u32[]{:S(2)}, u32[]{:S(2)}) collective-permute-start(bf16[104,768]{1,0:T(8,128)(2,1)S(1)} %concatenate.35), channel_id=1, source_target_pairs={{0,0},{1,4},{2,8},{3,12},{4,1},{5,5},{6,9},{7,13},{8,2},{9,6},{10,... | collective-permute-start | bytes 479240 | tf_op jit(solution)/shard_map/ppermute | solution.py:34
  15.8 5.0 %collective-permute-start.2 = (bf16[104,768]{1,0:T(8,128)(2,1)S(1)}, bf16[104,768]{1,0:T(8,128)(2,1)S(1)}, u32[]{:S(2)}, u32[]{:S(2)}) collective-permute-start(bf16[104,768]{1,0:T(8,128)(2,1)S(1)} %concatenate.35), channel_id=1, source_target_pairs={{0,2},{1,6},{2,10},{3,14},{4,3},{5,7},{6,11},{7,15},{8,0},{9,4},{1... | collective-permute-start | bytes 479240 | tf_op jit(solution)/shard_map/ppermute | solution.py:34
  22.5 3.6 %all-to-all-start = ((bf16[4,136,768]{2,1,0:T(8,128)(2,1)}), bf16[4,136,768]{2,1,0:T(8,128)(2,1)S(1)}, u32[]{:S(2)}, u32[]{:S(2)}) async-start(bf16[4,136,768]{2,1,0:T(8,128)(2,1)} %fusion.3), calls=%async_computation | async-start | bytes 1671168 | tf_op jit(solution)/shard_map/all_to_all | solution.py:61
  26.3 2.1 collective-permute-done.3
  29.8 18.0 %collective-permute-start.10 = (bf16[192,768]{1,0:T(8,128)(2,1)S(1)}, bf16[192,768]{1,0:T(8,128)(2,1)S(1)}, u32[]{:S(2)}, u32[]{:S(2)}) collective-permute-start(bf16[192,768]{1,0:T(8,128)(2,1)S(1)} %pad_maximum_fusion.4), channel_id=1, source_target_pairs={{0,0},{1,4},{2,8},{3,12},{4,1},{5,5},{6,9},{7,13},{8,2},{9,6},{10,... | collective-permute-start | bytes 884744 | tf_op jit(solution)/shard_map/ppermute | solution.py:34
  47.8 6.5 %collective-permute-done.10 = bf16[192,768]{1,0:T(8,128)(2,1)S(1)} collective-permute-done((bf16[192,768]{1,0:T(8,128)(2,1)S(1)}, bf16[192,768]{1,0:T(8,128)(2,1)S(1)}, u32[]{:S(2)}, u32[]{:S(2)}) %collective-permute-start.10) | collective-permute-done | bytes 294944 | tf_op jit(solution)/shard_map/ppermute | solution.py:34
  57.6 7.1 %collective-permute-done.5 = bf16[1,4,72,768]{3,2,1,0:T(8,128)(2,1)S(1)} collective-permute-done((bf16[1,4,72,768]{3,2,1,0:T(8,128)(2,1)S(1)}, bf16[1,4,72,768]{3,2,1,0:T(8,128)(2,1)S(1)}, u32[]{:S(2)}, u32[]{:S(2)}) %collective-permute-start.5) | collective-permute-done | bytes 442400 | tf_op jit(solution)/shard_map/ppermute | solution.py:26
  64.8 8.2 %collective-permute-start.6 = (bf16[2,4,72,768]{3,2,1,0:T(8,128)(2,1)S(1)}, bf16[2,4,72,768]{3,2,1,0:T(8,128)(2,1)S(1)}, u32[]{:S(2)}, u32[]{:S(2)}) collective-permute-start(bf16[2,4,72,768]{3,2,1,0:T(8,128)(2,1)S(1)} %pad_maximum_fusion.1.xo_ref.x_ref), channel_id=1, source_target_pairs={{0,4},{4,0},{8,12},{12,8},{1,5},{5,1},{9,13},{13,9},{2,6},{6,2},{1... | collective-permute-start | bytes 2654216 | tf_op jit(solution)/shard_map/ppermute | solution.py:26
  76.7 2.6 %qkv.1 = (bf16[4,4,64,768]{3,2,1,0:T(8,128)(2,1)S(1)}, f32[8,1024]{1,0:T(8,128)S(1)}, s32[4]{0:T(128)S(1)}, s32[4]{0:T(128)S(1)}) custom-call(bf16[2,4,72,768]{3,2,1,0:T(8,128)(2,1)S(1)} %pad_maximum_fusion.1.xo_ref.x_ref, bf16[2,4,72,768]{3,2,1,0:T(8,128)(2,1)S(1)} %collective-permute-done.6.xp_ref, f32[6,768]{1,0:T(8,128)S(1)} %stack.43.vec_ref, ...), custom_call_target="tpu_custom_call" | custom-call | flops 1080000000 | bytes 1024 | tf_op jit(solution)/shard_map/qkv/pallas_call | solution.py:174
  79.3 9.6 %attend.1 = (bf16[4,4,64,192]{3,2,1,0:T(8,128)(2,1)S(1)}, f32[8,1024]{1,0:T(8,128)S(1)}, f32[2,4,64,768]{3,2,1,0:T(8,128)S(1)}, bf16[2,4,64,768]{3,2,1,0:T(8,128)(2,1)S(1)}) custom-call(s32[4]{0:T(128)S(1)} %get-tuple-element.70.lo_ref, s32[4]{0:T(128)S(1)} %get-tuple-element.71.hi_ref, bf16[4,4,64,768]{3,2,1,0:T(8,128)(2,1)S(1)} %get-tuple-element.72.qkv_ref, ...), custom_call_target="tpu_custom_call" | custom-call | flops 2969999872 | bytes 1024 | tf_op jit(solution)/shard_map/attend/pallas_call | solution.py:337
  89.3 2.0 collective-permute-done.8.got_ref
  93.6 16.9 %collective-permute-done.9.got_ref = bf16[2,4,64,768]{3,2,1,0:T(8,128)(2,1)S(1)} collective-permute-done((bf16[2,4,64,768]{3,2,1,0:T(8,128)(2,1)S(1)}, bf16[2,4,64,768]{3,2,1,0:T(8,128)(2,1)S(1)}, u32[]{:S(2)}, u32[]{:S(2)}) %collective-permute-start.9) | collective-permute-done | bytes 786464 | tf_op jit(solution)/shard_map/ppermute | solution.py:26
  111.4 2.2 all-gather.2.cloned.1.call-done
  115.6 1.9 collective-permute-start.11
  119.5 4.2 %mlp_block.1 = (bf16[1024,768]{1,0:T(8,128)(2,1)S(1)}, bf16[1024,768]{1,0:T(8,128)(2,1)S(1)}, f32[2,4,64,768]{3,2,1,0:T(8,128)S(1)}, bf16[2,4,64,768]{3,2,1,0:T(8,128)(2,1)S(1)}) custom-call(bf16[2,4,64,768]{3,2,1,0:T(8,128)(2,1)S(1)} %get-tuple-element.83.xo_ref, bf16[2,4,64,768]{3,2,1,0:T(8,128)(2,1)S(1)} %collective-permute-done.11.xp_ref, ...), custom_call_target="tpu_custom_call" | custom-call | flops 1890000000 | bytes 1024 | tf_op jit(solution)/shard_map/mlp_block/pallas_call | solution.py:667
  124.2 1.9 collective-permute-done.13.got_ref
  127.6 5.9 %mlp_grads.1 = (bf16[4,2,2,96,768]{4,3,2,1,0:T(8,128)(2,1)S(1)}, f32[2,4,64,768]{3,2,1,0:T(8,128)S(1)}, bf16[2,4,64,768]{3,2,1,0:T(8,128)(2,1)}, f32[1,768]{1,0:T(1,128)S(1)}) custom-call(bf16[2,4,64,768]{3,2,1,0:T(8,128)(2,1)S(1)} %get-tuple-element.83.xo_ref, bf16[2,4,64,768]{3,2,1,0:T(8,128)(2,1)S(1)} %collective-permute-done.11.xp_ref, ...), custom_call_target="tpu_custom_call" | custom-call | flops 1620000000 | bytes 1024 | tf_op jit(solution)/shard_map/mlp_grads/pallas_call | solution.py:720
  133.5 11.7 %collective-permute-done.14.got_ref = bf16[2,4,64,768]{3,2,1,0:T(8,128)(2,1)S(1)} collective-permute-done((bf16[2,4,64,768]{3,2,1,0:T(8,128)(2,1)S(1)}, bf16[2,4,64,768]{3,2,1,0:T(8,128)(2,1)S(1)}, u32[]{:S(2)}, u32[]{:S(2)}) %collective-permute-start.14) | collective-permute-done | bytes 786464 | tf_op jit(solution)/shard_map/ppermute | solution.py:26
  146.3 2.4 middle_back.1
  154.9 15.5 %attend_back.1 = (bf16[4,4,64,768]{3,2,1,0:T(8,128)(2,1)S(1)}, f32[2,4,64,768]{3,2,1,0:T(8,128)S(1)}, bf16[2,4,64,768]{3,2,1,0:T(8,128)(2,1)S(1)}) custom-call(s32[4]{0:T(128)S(1)} %get-tuple-element.70.lo_ref, s32[4]{0:T(128)S(1)} %get-tuple-element.71.hi_ref, bf16[4,4,64,768]{3,2,1,0:T(8,128)(2,1)S(1)} %copy-done.17, ...), custom_call_target="tpu_custom_call" | custom-call | flops 18900000768 | bytes 1024 | tf_op jit(solution)/shard_map/attend_back/pallas_call | solution.py:459
  173.3 5.8 %attend_grads.1 = (bf16[392,768]{1,0:T(8,128)(2,1)S(1)}, bf16[392,768]{1,0:T(8,128)(2,1)}, f32[2,768]{1,0:T(2,128)S(1)}) custom-call(s32[1]{0:T(128)} %bitcast.14.flip_ref, f32[1,768]{1,0:T(1,128)S(1)} %get-tuple-element.90.sum_ref, f32[2,768]{1,0:T(2,128)S(1)} %get-tuple-element.171.norm_ref, bf16[1024,768]{1,0:T(8,128)(2,1)S(1)} %bitcast.64, ...), custom_call_target="tpu_custom_call" | custom-call | flops 1620000000 | bytes 1024 | tf_op jit(solution)/shard_map/attend_grads/pallas_call | solution.py:796
  179.3 3.0 %collective-permute-done.20 = f32[6,768]{1,0:T(8,128)S(1)} collective-permute-done((f32[6,768]{1,0:T(8,128)S(1)}, f32[6,768]{1,0:T(8,128)S(1)}, u32[]{:S(2)}, u32[]{:S(2)}) %collective-permute-start.20) | collective-permute-done | bytes 18464 | tf_op jit(solution)/shard_map/ppermute | solution.py:26
  186.5 3.5 %all-to-all-start.1 = ((bf16[4,128,768]{2,1,0:T(8,128)(2,1)}), bf16[4,128,768]{2,1,0:T(8,128)(2,1)S(1)}, u32[]{:S(2)}, u32[]{:S(2)}) async-start(bf16[4,128,768]{2,1,0:T(8,128)(2,1)} %first_back.1), calls=%async_computation.1 | async-start | bytes 1572864 | tf_op jit(solution)/shard_map/all_to_all | solution.py:61
  193.0 6.2 %collective-permute-done.22.got_ref = bf16[392,768]{1,0:T(8,128)(2,1)S(1)} collective-permute-done((bf16[392,768]{1,0:T(8,128)(2,1)}, bf16[392,768]{1,0:T(8,128)(2,1)S(1)}, u32[]{:S(2)}, u32[]{:S(2)}) %collective-permute-start.22) | collective-permute-done | bytes 602144 | tf_op jit(solution)/shard_map/ppermute | solution.py:26
  202.0 5.6 %collective-permute-done.24 = bf16[2,104,768]{2,1,0:T(8,128)(2,1)S(1)} collective-permute-done((bf16[2,104,768]{2,1,0:T(8,128)(2,1)S(1)}, bf16[2,104,768]{2,1,0:T(8,128)(2,1)S(1)}, u32[]{:S(2)}, u32[]{:S(2)}) %collective-permute-start.24) | collective-permute-done | bytes 319520 | tf_op jit(solution)/shard_map/ppermute | solution.py:26
  207.7 4.5 %all-to-all-done.1 = bf16[4,128,768]{2,1,0:T(8,128)(2,1)S(1)} async-done(((bf16[4,128,768]{2,1,0:T(8,128)(2,1)}), bf16[4,128,768]{2,1,0:T(8,128)(2,1)S(1)}, u32[]{:S(2)}, u32[]{:S(2)}) %all-to-all-start.1) | async-done | bytes 786464 | tf_op jit(solution)/shard_map/all_to_all | solution.py:61
  212.3 1.9 collective-permute-start.30
  214.3 3.6 %collective-permute-start.25 = (bf16[104,768]{1,0:T(8,128)(2,1)S(1)}, bf16[104,768]{1,0:T(8,128)(2,1)S(1)}, u32[]{:S(2)}, u32[]{:S(2)}) collective-permute-start(bf16[104,768]{1,0:T(8,128)(2,1)S(1)} %get-tuple-element.164), channel_id=1, source_target_pairs={{0,0},{1,4},{2,2},{3,6},{4,1},{5,5},{6,3},{7,7},{8,10},{9,14},{10,... | collective-permute-start | bytes 479240 | tf_op jit(solution)/shard_map/ppermute | solution.py:57
  218.0 4.6 %collective-permute-start.27 = (bf16[104,768]{1,0:T(8,128)(2,1)S(1)}, bf16[104,768]{1,0:T(8,128)(2,1)S(1)}, u32[]{:S(2)}, u32[]{:S(2)}) collective-permute-start(bf16[104,768]{1,0:T(8,128)(2,1)S(1)} %get-tuple-element.162), channel_id=1, source_target_pairs={{0,2},{1,6},{2,0},{3,4},{4,3},{5,7},{6,1},{7,5},{8,8},{9,12},{10,1... | collective-permute-start | bytes 479240 | tf_op jit(solution)/shard_map/ppermute | solution.py:57
  223.9 2.6 %collective-permute-done.25 = bf16[104,768]{1,0:T(8,128)(2,1)S(1)} collective-permute-done((bf16[104,768]{1,0:T(8,128)(2,1)S(1)}, bf16[104,768]{1,0:T(8,128)(2,1)S(1)}, u32[]{:S(2)}, u32[]{:S(2)}) %collective-permute-start.25) | collective-permute-done | bytes 159776 | tf_op jit(solution)/shard_map/ppermute | solution.py:57
  226.5 5.2 %collective-permute-done.27 = bf16[104,768]{1,0:T(8,128)(2,1)S(1)} collective-permute-done((bf16[104,768]{1,0:T(8,128)(2,1)S(1)}, bf16[104,768]{1,0:T(8,128)(2,1)S(1)}, u32[]{:S(2)}, u32[]{:S(2)}) %collective-permute-start.27) | collective-permute-done | bytes 159776 | tf_op jit(solution)/shard_map/ppermute | solution.py:57
  231.7 10.7 %collective-permute-done.28 = bf16[104,768]{1,0:T(8,128)(2,1)S(1)} collective-permute-done((bf16[104,768]{1,0:T(8,128)(2,1)S(1)}, bf16[104,768]{1,0:T(8,128)(2,1)S(1)}, u32[]{:S(2)}, u32[]{:S(2)}) %collective-permute-start.28) | collective-permute-done | bytes 159776 | tf_op jit(solution)/shard_map/ppermute | solution.py:57
  (175 shorter events, 50.1 us)
Async XLA Ops:
  11.1 15.1 %collective-permute-start = (bf16[104,768]{1,0:T(8,128)(2,1)S(1)}, bf16[104,768]{1,0:T(8,128)(2,1)S(1)}, u32[]{:S(2)}, u32[]{:S(2)}) collective-permute-start(bf16[104,768]{1,0:T(8,128)(2,1)S(1)} %concatenate.35), channel_id=1, source_target_pairs={{0,0},{1,4},{2,8},{3,12},{4,1},{5,5},{6,9},{7,13},{8,2},{9,6},{10,... | collective-permute-start | bytes 479240 | tf_op jit(solution)/shard_map/ppermute | solution.py:34
  15.7 10.5 %collective-permute-start.1 = (bf16[104,768]{1,0:T(8,128)(2,1)S(1)}, bf16[104,768]{1,0:T(8,128)(2,1)S(1)}, u32[]{:S(2)}, u32[]{:S(2)}) collective-permute-start(bf16[104,768]{1,0:T(8,128)(2,1)S(1)} %concatenate.35), channel_id=1, source_target_pairs={{0,1},{1,5},{2,9},{3,13},{4,0},{5,4},{6,8},{7,12},{8,3},{9,7},{10,... | collective-permute-start | bytes 479240 | tf_op jit(solution)/shard_map/ppermute | solution.py:34
  15.8 10.5 %collective-permute-start.2 = (bf16[104,768]{1,0:T(8,128)(2,1)S(1)}, bf16[104,768]{1,0:T(8,128)(2,1)S(1)}, u32[]{:S(2)}, u32[]{:S(2)}) collective-permute-start(bf16[104,768]{1,0:T(8,128)(2,1)S(1)} %concatenate.35), channel_id=1, source_target_pairs={{0,2},{1,6},{2,10},{3,14},{4,3},{5,7},{6,11},{7,15},{8,0},{9,4},{1... | collective-permute-start | bytes 479240 | tf_op jit(solution)/shard_map/ppermute | solution.py:34
  20.8 7.6 %collective-permute-start.3 = (bf16[104,768]{1,0:T(8,128)(2,1)S(1)}, bf16[104,768]{1,0:T(8,128)(2,1)S(1)}, u32[]{:S(2)}, u32[]{:S(2)}) collective-permute-start(bf16[104,768]{1,0:T(8,128)(2,1)S(1)} %concatenate.35), channel_id=1, source_target_pairs={{0,3},{1,7},{2,11},{3,15},{4,2},{5,6},{6,10},{7,14},{8,1},{9,5},{1... | collective-permute-start | bytes 479240 | tf_op jit(solution)/shard_map/ppermute | solution.py:34
  22.5 34.2 %all-to-all-start = ((bf16[4,136,768]{2,1,0:T(8,128)(2,1)}), bf16[4,136,768]{2,1,0:T(8,128)(2,1)S(1)}, u32[]{:S(2)}, u32[]{:S(2)}) async-start(bf16[4,136,768]{2,1,0:T(8,128)(2,1)} %fusion.3), calls=%async_computation | async-start | bytes 1671168 | tf_op jit(solution)/shard_map/all_to_all | solution.py:61
  26.1 87.4 %all-gather.2.cloned.1.call-start = ((), (), s32[]{:S(2)}) async-start(), calls=%async_computation.3 | async-start | bytes 2654208 | tf_op jit(solution)/shard_map/all_gather | solution.py:859
  28.5 26.7 %collective-permute-start.4 = (bf16[384,768]{1,0:T(8,128)(2,1)S(1)}, bf16[384,768]{1,0:T(8,128)(2,1)S(1)}, u32[]{:S(2)}, u32[]{:S(2)}) collective-permute-start(bf16[384,768]{1,0:T(8,128)(2,1)S(1)} %bitcast.67), channel_id=1, source_target_pairs={{0,16},{16,0},{1,17},{17,1},{2,18},{18,2},{3,19},{19,3},{4,20},{20... | collective-permute-start | bytes 1769480 | tf_op jit(solution)/shard_map/ppermute | solution.py:26
  29.8 24.6 %collective-permute-start.10 = (bf16[192,768]{1,0:T(8,128)(2,1)S(1)}, bf16[192,768]{1,0:T(8,128)(2,1)S(1)}, u32[]{:S(2)}, u32[]{:S(2)}) collective-permute-start(bf16[192,768]{1,0:T(8,128)(2,1)S(1)} %pad_maximum_fusion.4), channel_id=1, source_target_pairs={{0,0},{1,4},{2,8},{3,12},{4,1},{5,5},{6,9},{7,13},{8,2},{9,6},{10,... | collective-permute-start | bytes 884744 | tf_op jit(solution)/shard_map/ppermute | solution.py:34
  55.1 145.7 %reduce-scatter.2.cloned.1.call-start = ((), (), s32[]{:S(2)}) async-start(), calls=%async_computation.4 | async-start | bytes 2949120 | tf_op jit(solution)/shard_map/reduce_scatter | solution.py:891
  56.7 8.0 %collective-permute-start.5 = (bf16[1,4,72,768]{3,2,1,0:T(8,128)(2,1)S(1)}, bf16[1,4,72,768]{3,2,1,0:T(8,128)(2,1)S(1)}, u32[]{:S(2)}, u32[]{:S(2)}) collective-permute-start(bf16[1,4,72,768]{3,2,1,0:T(8,128)(2,1)S(1)} %bitcast.68), channel_id=1, source_target_pairs={{0,8},{4,12},{8,0},{12,4},{1,9},{5,13},{9,1},{13,5},{2,10},{6,14},... | collective-permute-start | bytes 1327112 | tf_op jit(solution)/shard_map/ppermute | solution.py:26
  64.8 11.9 %collective-permute-start.6 = (bf16[2,4,72,768]{3,2,1,0:T(8,128)(2,1)S(1)}, bf16[2,4,72,768]{3,2,1,0:T(8,128)(2,1)S(1)}, u32[]{:S(2)}, u32[]{:S(2)}) collective-permute-start(bf16[2,4,72,768]{3,2,1,0:T(8,128)(2,1)S(1)} %pad_maximum_fusion.1.xo_ref.x_ref), channel_id=1, source_target_pairs={{0,4},{4,0},{8,12},{12,8},{1,5},{5,1},{9,13},{13,9},{2,6},{6,2},{1... | collective-permute-start | bytes 2654216 | tf_op jit(solution)/shard_map/ppermute | solution.py:26
  74.8 14.2 %collective-permute-start.7 = (bf16[1,4,64,768]{3,2,1,0:T(8,128)(2,1)}, bf16[1,4,64,768]{3,2,1,0:T(8,128)(2,1)}, u32[]{:S(2)}, u32[]{:S(2)}) collective-permute-start(bf16[1,4,64,768]{3,2,1,0:T(8,128)(2,1)} %bitcast.11), channel_id=1, source_target_pairs={{0,8},{4,12},{8,0},{12,4},{1,9},{5,13},{9,1},{13,5},{2,10},{6,14},... | collective-permute-start | bytes 1179656 | tf_op jit(solution)/shard_map/ppermute | solution.py:26
  91.5 19.0 %collective-permute-start.9 = (bf16[2,4,64,768]{3,2,1,0:T(8,128)(2,1)S(1)}, bf16[2,4,64,768]{3,2,1,0:T(8,128)(2,1)S(1)}, u32[]{:S(2)}, u32[]{:S(2)}) collective-permute-start(bf16[2,4,64,768]{3,2,1,0:T(8,128)(2,1)S(1)} %add_rows.4.s_ref), channel_id=1, source_target_pairs={{0,8},{4,12},{8,0},{12,4},{1,9},{5,13},{9,1},{13,5},{2,10},{6,14},... | collective-permute-start | bytes 2359304 | tf_op jit(solution)/shard_map/ppermute | solution.py:26
  92.9 24.7 %collective-permute-start.12 = (bf16[2,4,64,768]{3,2,1,0:T(8,128)(2,1)S(1)}, bf16[2,4,64,768]{3,2,1,0:T(8,128)(2,1)S(1)}, u32[]{:S(2)}, u32[]{:S(2)}) collective-permute-start(bf16[2,4,64,768]{3,2,1,0:T(8,128)(2,1)S(1)} %pad_maximum_fusion.2.go_ref.g_ref), channel_id=1, source_target_pairs={{0,4},{4,0},{8,12},{12,8},{1,5},{5,1},{9,13},{13,9},{2,6},{6,2},{1... | collective-permute-start | bytes 2359304 | tf_op jit(solution)/shard_map/ppermute | solution.py:26
  115.6 3.8 %collective-permute-start.11 = (bf16[2,4,64,768]{3,2,1,0:T(8,128)(2,1)S(1)}, bf16[2,4,64,768]{3,2,1,0:T(8,128)(2,1)S(1)}, u32[]{:S(2)}, u32[]{:S(2)}) collective-permute-start(bf16[2,4,64,768]{3,2,1,0:T(8,128)(2,1)S(1)} %get-tuple-element.83.xo_ref), channel_id=1, source_target_pairs={{0,4},{4,0},{8,12},{12,8},{1,5},{5,1},{9,13},{13,9},{2,6},{6,2},{1... | collective-permute-start | bytes 2359304 | tf_op jit(solution)/shard_map/ppermute | solution.py:26
  126.3 18.8 %collective-permute-start.14 = (bf16[2,4,64,768]{3,2,1,0:T(8,128)(2,1)S(1)}, bf16[2,4,64,768]{3,2,1,0:T(8,128)(2,1)S(1)}, u32[]{:S(2)}, u32[]{:S(2)}) collective-permute-start(bf16[2,4,64,768]{3,2,1,0:T(8,128)(2,1)S(1)} %add_rows.5.s_ref), channel_id=1, source_target_pairs={{0,8},{4,12},{8,0},{12,4},{1,9},{5,13},{9,1},{13,5},{2,10},{6,14},... | collective-permute-start | bytes 2359304 | tf_op jit(solution)/shard_map/ppermute | solution.py:26
  145.1 4.6 %collective-permute-start.16 = (bf16[2,4,64,768]{3,2,1,0:T(8,128)(2,1)}, bf16[2,4,64,768]{3,2,1,0:T(8,128)(2,1)}, u32[]{:S(2)}, u32[]{:S(2)}) collective-permute-start(bf16[2,4,64,768]{3,2,1,0:T(8,128)(2,1)} %get-tuple-element.98), channel_id=1, source_target_pairs={{0,4},{4,0},{8,12},{12,8},{1,5},{5,1},{9,13},{13,9},{2,6},{6,2},{1... | collective-permute-start | bytes 2359304 | tf_op jit(solution)/shard_map/ppermute | solution.py:26
  149.7 2.5 collective-permute-start.15
  152.2 18.2 %collective-permute-start.17 = (bf16[1,4,64,768]{3,2,1,0:T(8,128)(2,1)S(1)}, bf16[1,4,64,768]{3,2,1,0:T(8,128)(2,1)S(1)}, u32[]{:S(2)}, u32[]{:S(2)}) collective-permute-start(bf16[1,4,64,768]{3,2,1,0:T(8,128)(2,1)S(1)} %get-tuple-element.100), channel_id=1, source_target_pairs={{0,8},{4,12},{8,0},{12,4},{1,9},{5,13},{9,1},{13,5},{2,10},{6,14},... | collective-permute-start | bytes 1179656 | tf_op jit(solution)/shard_map/ppermute | solution.py:26
  170.4 2.6 %collective-permute-start.18 = (bf16[2,4,64,768]{3,2,1,0:T(8,128)(2,1)S(1)}, bf16[2,4,64,768]{3,2,1,0:T(8,128)(2,1)S(1)}, u32[]{:S(2)}, u32[]{:S(2)}) collective-permute-start(bf16[2,4,64,768]{3,2,1,0:T(8,128)(2,1)S(1)} %get-tuple-element.101.sent_ref), channel_id=1, source_target_pairs={{0,4},{4,0},{8,12},{12,8},{1,5},{5,1},{9,13},{13,9},{2,6},{6,2},{1... | collective-permute-start | bytes 2359304 | tf_op jit(solution)/shard_map/ppermute | solution.py:26
  173.1 11.5 %collective-permute-start.19 = (bf16[1,4,64,768]{3,2,1,0:T(8,128)(2,1)S(1)}, bf16[1,4,64,768]{3,2,1,0:T(8,128)(2,1)S(1)}, u32[]{:S(2)}, u32[]{:S(2)}) collective-permute-start(bf16[1,4,64,768]{3,2,1,0:T(8,128)(2,1)S(1)} %get-tuple-element.103), channel_id=1, source_target_pairs={{0,8},{4,12},{8,0},{12,4},{1,9},{5,13},{9,1},{13,5},{2,10},{6,14},... | collective-permute-start | bytes 1179656 | tf_op jit(solution)/shard_map/ppermute | solution.py:26
  179.2 3.1 %collective-permute-start.20 = (f32[6,768]{1,0:T(8,128)S(1)}, f32[6,768]{1,0:T(8,128)S(1)}, u32[]{:S(2)}, u32[]{:S(2)}) collective-permute-start(f32[6,768]{1,0:T(8,128)S(1)} %pad_maximum_fusion.6), channel_id=1, source_target_pairs={{0,16},{16,0},{1,17},{17,1},{2,18},{18,2},{3,19},{19,3},{4,20},{20... | collective-permute-start | bytes 55304 | tf_op jit(solution)/shard_map/ppermute | solution.py:26
  183.8 15.4 %collective-permute-start.22 = (bf16[392,768]{1,0:T(8,128)(2,1)}, bf16[392,768]{1,0:T(8,128)(2,1)S(1)}, u32[]{:S(2)}, u32[]{:S(2)}) collective-permute-start(bf16[392,768]{1,0:T(8,128)(2,1)} %get-tuple-element.112), channel_id=1, source_target_pairs={{0,16},{16,0},{1,17},{17,1},{2,18},{18,2},{3,19},{19,3},{4,20},{20... | collective-permute-start | bytes 1806344 | tf_op jit(solution)/shard_map/ppermute | solution.py:26
  186.5 25.7 %all-to-all-start.1 = ((bf16[4,128,768]{2,1,0:T(8,128)(2,1)}), bf16[4,128,768]{2,1,0:T(8,128)(2,1)S(1)}, u32[]{:S(2)}, u32[]{:S(2)}) async-start(bf16[4,128,768]{2,1,0:T(8,128)(2,1)} %first_back.1), calls=%async_computation.1 | async-start | bytes 1572864 | tf_op jit(solution)/shard_map/all_to_all | solution.py:61
  190.0 3.0 %collective-permute-start.23 = (f32[6,768]{1,0:T(8,128)S(1)}, f32[6,768]{1,0:T(8,128)S(1)}, u32[]{:S(2)}, u32[]{:S(2)}) collective-permute-start(f32[6,768]{1,0:T(8,128)S(1)} %add.65), channel_id=1, source_target_pairs={{0,8},{4,12},{8,0},{12,4},{1,9},{5,13},{9,1},{13,5},{2,10},{6,14},... | collective-permute-start | bytes 55304 | tf_op jit(solution)/shard_map/ppermute | solution.py:26
  199.4 8.3 %collective-permute-start.24 = (bf16[2,104,768]{2,1,0:T(8,128)(2,1)S(1)}, bf16[2,104,768]{2,1,0:T(8,128)(2,1)S(1)}, u32[]{:S(2)}, u32[]{:S(2)}) collective-permute-start(bf16[2,104,768]{2,1,0:T(8,128)(2,1)S(1)} %get-tuple-element.166), channel_id=1, source_target_pairs={{0,8},{4,12},{8,0},{12,4},{1,9},{5,13},{9,1},{13,5},{2,10},{6,14},... | collective-permute-start | bytes 958472 | tf_op jit(solution)/shard_map/ppermute | solution.py:26
  201.8 10.4 %collective-permute-start.29 = (bf16[2,96,768]{2,1,0:T(8,128)(2,1)S(1)}, bf16[2,96,768]{2,1,0:T(8,128)(2,1)S(1)}, u32[]{:S(2)}, u32[]{:S(2)}) collective-permute-start(bf16[2,96,768]{2,1,0:T(8,128)(2,1)S(1)} %dynamic-slice_bitcast_fusion.2), channel_id=1, source_target_pairs={{0,16},{16,0},{1,17},{17,1},{2,18},{18,2},{3,19},{19,3},{4,20},{20... | collective-permute-start | bytes 884744 | tf_op jit(solution)/shard_map/ppermute | solution.py:26
  212.3 30.1 %collective-permute-start.30 = (bf16[192,768]{1,0:T(8,128)(2,1)S(1)}, bf16[192,768]{1,0:T(8,128)(2,1)S(1)}, u32[]{:S(2)}, u32[]{:S(2)}) collective-permute-start(bf16[192,768]{1,0:T(8,128)(2,1)S(1)} %bitcast.73), channel_id=1, source_target_pairs={{0,0},{4,1},{8,2},{12,3},{1,4},{5,5},{9,6},{13,7},{2,8},{6,9},{10,... | collective-permute-start | bytes 884744 | tf_op jit(solution)/shard_map/ppermute | solution.py:39
  214.3 12.2 %collective-permute-start.25 = (bf16[104,768]{1,0:T(8,128)(2,1)S(1)}, bf16[104,768]{1,0:T(8,128)(2,1)S(1)}, u32[]{:S(2)}, u32[]{:S(2)}) collective-permute-start(bf16[104,768]{1,0:T(8,128)(2,1)S(1)} %get-tuple-element.164), channel_id=1, source_target_pairs={{0,0},{1,4},{2,2},{3,6},{4,1},{5,5},{6,3},{7,7},{8,10},{9,14},{10,... | collective-permute-start | bytes 479240 | tf_op jit(solution)/shard_map/ppermute | solution.py:57
  217.9 8.6 %collective-permute-start.26 = (bf16[104,768]{1,0:T(8,128)(2,1)S(1)}, bf16[104,768]{1,0:T(8,128)(2,1)S(1)}, u32[]{:S(2)}, u32[]{:S(2)}) collective-permute-start(bf16[104,768]{1,0:T(8,128)(2,1)S(1)} %get-tuple-element.163), channel_id=1, source_target_pairs={{0,4},{1,0},{2,6},{3,2},{4,5},{5,1},{6,7},{7,3},{8,14},{9,10},{10,... | collective-permute-start | bytes 479240 | tf_op jit(solution)/shard_map/ppermute | solution.py:57
  218.0 13.7 %collective-permute-start.27 = (bf16[104,768]{1,0:T(8,128)(2,1)S(1)}, bf16[104,768]{1,0:T(8,128)(2,1)S(1)}, u32[]{:S(2)}, u32[]{:S(2)}) collective-permute-start(bf16[104,768]{1,0:T(8,128)(2,1)S(1)} %get-tuple-element.162), channel_id=1, source_target_pairs={{0,2},{1,6},{2,0},{3,4},{4,3},{5,7},{6,1},{7,5},{8,8},{9,12},{10,1... | collective-permute-start | bytes 479240 | tf_op jit(solution)/shard_map/ppermute | solution.py:57
  222.6 19.8 %collective-permute-start.28 = (bf16[104,768]{1,0:T(8,128)(2,1)S(1)}, bf16[104,768]{1,0:T(8,128)(2,1)S(1)}, u32[]{:S(2)}, u32[]{:S(2)}) collective-permute-start(bf16[104,768]{1,0:T(8,128)(2,1)S(1)} %get-tuple-element.161), channel_id=1, source_target_pairs={{0,6},{1,2},{2,4},{3,0},{4,7},{5,3},{6,5},{7,1},{8,12},{9,8},{10,1... | collective-permute-start | bytes 479240 | tf_op jit(solution)/shard_map/ppermute | solution.py:57
  (34 other events, 326.0 us)
Sparse Core Ops, SparseCore 0:
  55.2 58.2 all-gather.1
  149.8 46.2 reduce-scatter.1
